TPU v7x, 32 devices: a whole 2x2x4 slice. The times are simulated.
32 devices in a mesh: groups: 2 (over x), seq: 16 (over z, y, core).
Axes of the slice: x: 2, y: 2, z: 4, core: 2. Of those that a mesh axis runs over, the one named last changes fastest.
Arguments:
- queries: bfloat16 [64, 4, 8192], P(('groups', 'seq')), parts along dimension 0, may hold values from -128 to 128
- step_keys: bfloat16 [64, 4, 1024], P(('groups', 'seq')), parts along dimension 0, may hold values from -15 to 15
- step_values: bfloat16 [64, 4, 1024], P(('groups', 'seq')), parts along dimension 0, may hold values from -48 to 48
- sample_keys: bfloat16 [64, 1024, 1024], P(('groups', 'seq')), parts along dimension 0, may hold values from -6 to 6
- sample_values: bfloat16 [64, 1024, 1024], P(('groups', 'seq')), parts along dimension 0, may hold values from -48 to 48
- suffix_len: int32 [64], P(('groups', 'seq')), parts along dimension 0, may hold values from 128 to 1024
- prompt_id: int32 [64], P(('groups', 'seq')), parts along dimension 0, may hold values from 0 to 1, as said below
- document_keys: bfloat16 [4, 4096, 1024], P('groups', 'seq'), parts along dimension 0, may hold values from -6 to 6
- document_values: bfloat16 [4, 4096, 1024], P('groups', 'seq'), parts along dimension 0, may hold values from -48 to 48
Outputs:
- attended: bfloat16 [64, 4, 8192], P(('groups', 'seq')), parts along dimension 0
There are 2 independent parts, one for each index of `groups`. A program takes and returns all parts, laid end to end along the dimension named above; each array names one. Nothing has to cross between parts.
Inputs may be any that keep to these rules, and one draw needn't show every extreme that they name: `prompt_id`: each prompt id is held by exactly 16 samples.
All inputs are finite; a program needn't handle non-finite values.
Results may differ from a plain program's by a relative error of at most 0.0013.
Values may be sent and summed in bfloat16 or wider, within the bound.
A program may use at most 192 MiB of HBM per device.

v0:
```python
import functools

import jax
import jax.numpy as jnp
from jax import lax
from jax.experimental import pallas as pl
from jax.experimental.pallas import tpu as pltpu
from jax.sharding import PartitionSpec as P

QUERY_HEADS = 64
KEY_VALUE_HEADS = 8
HEAD_SIZE = 128
LOG2E = 1.4426950408889634
ID_ROWS = 16
STAT_ROWS = 8
MESH = pl.DeviceIdType.MESH
NT = (((1,), (1,)), ((), ()))
NN = (((1,), (0,)), ((), ()))


def member(head, offset):
    result = 0
    for bit in range(3):
        weight = 1 << bit
        own = lax.rem(head // weight, 2)
        result = result + weight * (1 - own if offset & weight else own)
    return result


def kernel(
    n,
    len_ref,
    query_ref,
    step_key_ref,
    step_value_ref,
    sample_keys,
    sample_values,
    document_keys,
    document_values,
    out_ref,
    key_buf,
    value_buf,
    head_keys,
    head_values,
    query_buf,
    query_cat,
    id_buf,
    acc,
    acc_max,
    acc_total,
    send_buf,
    got_buf,
    own_out,
    own_max,
    own_total,
    local_sem,
    query_send,
    query_recv,
    pair_send,
    pair_recv,
    part_send,
    part_recv,
):
    me = lax.axis_index("seq")
    my_head = lax.rem(me, KEY_VALUE_HEADS)
    my_base = me - my_head
    samples, cache = sample_keys.shape[0], sample_keys.shape[1]
    steps = step_key_ref.shape[1]
    rows = query_ref.shape[2] - ID_ROWS
    owner_rows = samples * rows
    prompts = document_keys.shape[0]
    padded = key_buf.shape[1]
    factor = (HEAD_SIZE ** (-0.5)) * LOG2E

    def columns(head):
        return pl.ds(pl.multiple_of(head * HEAD_SIZE, HEAD_SIZE), HEAD_SIZE)

    local = [
        pltpu.make_async_copy(
            sample_keys, key_buf.at[:, pl.ds(0, cache), :], local_sem.at[0]
        ),
        pltpu.make_async_copy(
            sample_values, value_buf.at[:, pl.ds(0, cache), :], local_sem.at[1]
        ),
        pltpu.make_async_copy(
            document_keys.at[:, :, columns(my_head)], head_keys.at[0], local_sem.at[2]
        ),
        pltpu.make_async_copy(
            document_values.at[:, :, columns(my_head)], head_values.at[0], local_sem.at[3]
        ),
    ]
    for copy in local:
        copy.start()

    barrier = pltpu.get_barrier_semaphore()

    def greet(step, carry):
        other = lax.rem(me + step, n)
        pl.semaphore_signal(barrier, inc=1, device_id={"seq": other}, device_id_type=MESH)
        return carry

    lax.fori_loop(1, n, greet, 0)
    pl.semaphore_wait(barrier, n - 1)

    def send_query(step, carry):
        other = lax.rem(me + step, n)
        pltpu.make_async_remote_copy(
            src_ref=query_ref.at[lax.rem(other, KEY_VALUE_HEADS)],
            dst_ref=query_buf.at[me],
            send_sem=query_send,
            recv_sem=query_recv,
            device_id={"seq": other},
            device_id_type=MESH,
        ).start()
        return carry

    lax.fori_loop(1, n, send_query, 0)

    pairs = {}
    for offset in (2, 4, 3, 5, 6, 7, 1):
        head = member(my_head, offset)
        for kind, (source, target) in enumerate(
            ((document_keys, head_keys), (document_values, head_values))
        ):
            copy = pltpu.make_async_remote_copy(
                src_ref=source.at[:, :, columns(head)],
                dst_ref=target.at[offset],
                send_sem=pair_send.at[kind, offset],
                recv_sem=pair_recv.at[kind, offset],
                device_id={"seq": my_base + head},
                device_id_type=MESH,
            )
            copy.start()
            pairs[kind, offset] = copy

    query_buf[me] = query_ref[my_head]
    for s in range(samples):
        key_buf[s, pl.ds(cache, padded - cache), :] = jnp.zeros(
            (padded - cache, key_buf.shape[2]), key_buf.dtype
        )
        value_buf[s, pl.ds(cache, padded - cache), :] = jnp.zeros(
            (padded - cache, value_buf.shape[2]), value_buf.dtype
        )
        key_buf[s, pl.ds(cache, steps), :] = step_key_ref[s]
        value_buf[s, pl.ds(cache, steps), :] = step_value_ref[s]
    for copy in local:
        copy.wait()

    slot = lax.broadcasted_iota(jnp.int32, (rows, padded), 1)
    now = lax.broadcasted_iota(jnp.int32, (rows, padded), 0) // (rows // steps)
    fresh = (slot >= cache) & (slot - cache <= now)

    def suffix_head(head, carry):
        for s in range(samples):
            query = query_ref[head, s, pl.ds(0, rows), :]
            scores = lax.dot_general(
                query, key_buf[s, :, columns(head)], NT, preferred_element_type=jnp.float32
            )
            live = (slot < len_ref[s]) | fresh
            scores = jnp.where(live, scores, -jnp.inf)
            peak = jnp.max(scores, axis=1, keepdims=True)
            expo = jnp.exp2((scores - peak) * factor)
            part = pl.ds(s * rows, rows)
            own_max[head, part, :] = peak
            own_total[head, part, :] = jnp.sum(expo, axis=1, keepdims=True)
            own_out[head, part, :] = lax.dot_general(
                expo.astype(jnp.bfloat16),
                value_buf[s, :, columns(head)],
                NN,
                preferred_element_type=jnp.float32,
            )
        return carry

    lax.fori_loop(0, KEY_VALUE_HEADS, suffix_head, 0)

    others = query_buf.at[pl.ds(0, n - 1)]
    pltpu.make_async_copy(others, others, query_recv).wait()

    def place(source, carry):
        for s in range(samples):
            query = query_buf[source, s, pl.ds(0, rows), :].astype(jnp.float32)
            mark = query_buf[source, s, pl.ds(rows, ID_ROWS), :].astype(jnp.float32)
            mark = jnp.concatenate([mark] * (rows // ID_ROWS), axis=0)
            part = pl.ds(pl.multiple_of(source * owner_rows + s * rows, rows), rows)
            for p in range(prompts):
                query_cat[part, pl.ds(p * HEAD_SIZE, HEAD_SIZE)] = jnp.where(
                    mark == p, query, 0.0
                ).astype(jnp.bfloat16)
            id_buf[part, :] = mark
            acc[part, :] = jnp.zeros((rows, HEAD_SIZE), jnp.float32)
            acc_max[part, :] = jnp.full((rows, 1), -1e30, jnp.float32)
            acc_total[part, :] = jnp.zeros((rows, 1), jnp.float32)
        return carry

    lax.fori_loop(0, n, place, 0)

    owners = 4 if n % 4 == 0 else 1
    chunk = owners * owner_rows

    def attend(offset, index):
        part = pl.ds(pl.multiple_of(index * chunk, chunk), chunk)
        keys = jnp.concatenate([head_keys[offset, p] for p in range(prompts)], axis=1)
        values = jnp.concatenate([head_values[offset, p] for p in range(prompts)], axis=1)
        scores = lax.dot_general(
            query_cat[part, :], keys, NT, preferred_element_type=jnp.float32
        )
        peak = jnp.max(scores, axis=1, keepdims=True)
        expo = jnp.exp2((scores - peak) * factor)
        total = jnp.sum(expo, axis=1, keepdims=True)
        both = lax.dot_general(
            expo.astype(jnp.bfloat16), values, NN, preferred_element_type=jnp.float32
        )
        mark = id_buf[part, :]
        result = both[:, :HEAD_SIZE]
        for p in range(1, prompts):
            result = jnp.where(
                mark == p, both[:, p * HEAD_SIZE : (p + 1) * HEAD_SIZE], result
            )
        before = acc_max[part, :]
        top = jnp.maximum(before, peak)
        old = jnp.exp2((before - top) * factor)
        new = jnp.exp2((peak - top) * factor)
        return part, acc[part, :] * old + result * new, top, acc_total[part, :] * old + total * new

    def keep(offset, index):
        part, merged, top, total = attend(offset, index)
        acc[part, :] = merged
        acc_max[part, :] = top
        acc_total[part, :] = total

    def over_block(offset, carry):
        lax.fori_loop(0, n // owners, lambda i, c: (keep(offset, i), c)[1], 0)
        return carry

    over_block(0, 0)
    last = KEY_VALUE_HEADS - 1
    for offset in range(1, last):
        pairs[0, offset].wait_recv()
        pairs[1, offset].wait_recv()
        over_block(offset, 0)
    pairs[0, last].wait_recv()
    pairs[1, last].wait_recv()

    diagonal = lax.broadcasted_iota(jnp.int32, (owner_rows, HEAD_SIZE), 0) == (
        lax.broadcasted_iota(jnp.int32, (owner_rows, HEAD_SIZE), 1)
    )
    stat_row = lax.broadcasted_iota(jnp.int32, (STAT_ROWS, HEAD_SIZE), 0)

    chunks = n // owners

    def finish(step, carry):
        index = lax.rem(me // owners + chunks // 2 + step, chunks)
        _, merged, top, total = attend(last, index)
        for j in range(owners):
            owner = index * owners + j
            cut = slice(j * owner_rows, (j + 1) * owner_rows)
            send_buf[owner, pl.ds(0, owner_rows), :] = merged[cut]
            peak_row = jnp.sum(jnp.where(diagonal, top[cut], 0.0), axis=0, keepdims=True)
            total_row = jnp.sum(jnp.where(diagonal, total[cut], 0.0), axis=0, keepdims=True)
            send_buf[owner, pl.ds(owner_rows, STAT_ROWS), :] = jnp.where(
                stat_row == 0, peak_row, jnp.where(stat_row == 1, total_row, 0.0)
            )

            @pl.when(owner != me)
            def _():
                pltpu.make_async_remote_copy(
                    src_ref=send_buf.at[owner],
                    dst_ref=got_buf.at[me],
                    send_sem=part_send,
                    recv_sem=part_recv,
                    device_id={"seq": owner},
                    device_id_type=MESH,
                ).start()

        return carry

    lax.fori_loop(0, n // owners, finish, 0)
    got_buf[me] = send_buf[me]
    others = got_buf.at[pl.ds(0, n - 1)]
    pltpu.make_async_copy(others, others, part_recv).wait()

    def merge(head, carry):
        top = own_max[head]
        parts = []
        for group in range(n // KEY_VALUE_HEADS):
            source = group * KEY_VALUE_HEADS + head
            stats = got_buf[source, pl.ds(owner_rows, STAT_ROWS), :]
            peak = jnp.sum(jnp.where(diagonal, stats[0:1], 0.0), axis=1, keepdims=True)
            total = jnp.sum(jnp.where(diagonal, stats[1:2], 0.0), axis=1, keepdims=True)
            parts.append((source, peak, total))
            top = jnp.maximum(top, peak)
        weight = jnp.exp2((own_max[head] - top) * factor)
        above = own_out[head] * weight
        below = own_total[head] * weight
        for source, peak, total in parts:
            weight = jnp.exp2((peak - top) * factor)
            above = above + got_buf[source, pl.ds(0, owner_rows), :] * weight
            below = below + total * weight
        out_ref[head] = (above / below).astype(out_ref.dtype)
        return carry

    lax.fori_loop(0, KEY_VALUE_HEADS, merge, 0)

    sent = query_buf.at[pl.ds(0, n - 1)]
    pltpu.make_async_copy(sent, sent, query_send).wait()
    sent = send_buf.at[pl.ds(0, n - 1)]
    pltpu.make_async_copy(sent, sent, part_send).wait()
    for copy in pairs.values():
        copy.wait_send()


def body(
    queries,
    step_keys,
    step_values,
    sample_keys,
    sample_values,
    suffix_len,
    prompt_id,
    document_keys,
    document_values,
):
    n = lax.axis_size("seq")
    samples, steps = queries.shape[:2]
    cache = sample_keys.shape[1]
    width = KEY_VALUE_HEADS * HEAD_SIZE
    prompts, block = document_keys.shape[:2]
    group = QUERY_HEADS // KEY_VALUE_HEADS
    rows = steps * group
    owner_rows = samples * rows
    total_rows = n * owner_rows
    padded = cache + 128
    by_head = queries.reshape(samples, steps, KEY_VALUE_HEADS, group, HEAD_SIZE)
    by_head = by_head.transpose(2, 0, 1, 3, 4).reshape(KEY_VALUE_HEADS, samples, rows, HEAD_SIZE)
    marks = jnp.broadcast_to(
        prompt_id.astype(jnp.bfloat16)[None, :, None, None],
        (KEY_VALUE_HEADS, samples, ID_ROWS, HEAD_SIZE),
    )
    messages = jnp.concatenate([by_head, marks], axis=2)
    f32, bf16 = jnp.float32, jnp.bfloat16
    vmem = pl.BlockSpec(memory_space=pltpu.VMEM)
    hbm = pl.BlockSpec(memory_space=pl.ANY)
    dma = pltpu.SemaphoreType.DMA
    result = pl.pallas_call(
        functools.partial(kernel, n),
        out_shape=jax.ShapeDtypeStruct((KEY_VALUE_HEADS, owner_rows, HEAD_SIZE), bf16),
        in_specs=[pl.BlockSpec(memory_space=pltpu.SMEM), vmem, vmem, vmem, hbm, hbm, hbm, hbm],
        out_specs=vmem,
        scratch_shapes=[
            pltpu.VMEM((samples, padded, width), bf16),
            pltpu.VMEM((samples, padded, width), bf16),
            pltpu.VMEM((KEY_VALUE_HEADS, prompts, block, HEAD_SIZE), bf16),
            pltpu.VMEM((KEY_VALUE_HEADS, prompts, block, HEAD_SIZE), bf16),
            pltpu.VMEM((n, samples, rows + ID_ROWS, HEAD_SIZE), bf16),
            pltpu.VMEM((total_rows, prompts * HEAD_SIZE), bf16),
            pltpu.VMEM((total_rows, HEAD_SIZE), f32),
            pltpu.VMEM((total_rows, HEAD_SIZE), f32),
            pltpu.VMEM((total_rows, 1), f32),
            pltpu.VMEM((total_rows, 1), f32),
            pltpu.VMEM((n, owner_rows + STAT_ROWS, HEAD_SIZE), f32),
            pltpu.VMEM((n, owner_rows + STAT_ROWS, HEAD_SIZE), f32),
            pltpu.VMEM((KEY_VALUE_HEADS, owner_rows, HEAD_SIZE), f32),
            pltpu.VMEM((KEY_VALUE_HEADS, owner_rows, 1), f32),
            pltpu.VMEM((KEY_VALUE_HEADS, owner_rows, 1), f32),
            dma((4,)),
            dma,
            dma,
            dma((2, KEY_VALUE_HEADS)),
            dma((2, KEY_VALUE_HEADS)),
            dma,
            dma,
        ],
        compiler_params=pltpu.CompilerParams(
            collective_id=0, has_side_effects=True, vmem_limit_bytes=60 << 20
        ),
    )(
        suffix_len,
        messages,
        step_keys,
        step_values,
        sample_keys,
        sample_values,
        document_keys,
        document_values,
    )
    result = result.reshape(KEY_VALUE_HEADS, samples, steps, group, HEAD_SIZE)
    return result.transpose(1, 2, 0, 3, 4).reshape(samples, steps, QUERY_HEADS * HEAD_SIZE)


def solution(mesh):
    return jax.shard_map(
        body,
        mesh=mesh,
        in_specs=(
            P(("groups", "seq"), None, None),
            P(("groups", "seq"), None, None),
            P(("groups", "seq"), None, None),
            P(("groups", "seq"), None, None),
            P(("groups", "seq"), None, None),
            P(("groups", "seq")),
            P(("groups", "seq")),
            P("groups", "seq", None),
            P("groups", "seq", None),
        ),
        out_specs=P(("groups", "seq"), None, None),
        check_vma=False,
    )
```

profile of v0, /device:TPU:0, one launch (start us, length us, event | category | flops | bytes accessed | tf_op | source)
XLA Modules:
  0.0 60.1 jit_solution(5924288328499319482)
XLA Ops:
  0.0 0.7 %convert_element_type.3 = bf16[2]{0:T(256)(128)(2,1)S(1)} convert(s32[2]{0:T(128)} %param.15) | non-fusion elementwise | flops 2 | bytes 12 | tf_op jit(solution)/shard_map/convert_element_type | solution.py:336
  0.7 0.1 broadcast_in_dim.2
  0.7 1.1 %reshape.13 = bf16[2,4,8,8,128]{4,3,2,1,0:T(8,128)(2,1)S(1)} reshape(bf16[2,4,8192]{2,1,0:T(4,128)(2,1)} %param.9) | data formatting | bytes 262144 | tf_op jit(solution)/shard_map/reshape | solution.py:333
  1.8 0.7 %pad_maximum_fusion.query_ref = bf16[8,2,48,128]{3,2,1,0:T(8,128)(2,1)} fusion(bf16[8,2,16,128]{3,2,1,0:T(8,128)(2,1)S(1)} %broadcast_in_dim.2, bf16[8,2,32,128]{3,2,1,0:T(8,128)(2,1)S(1)} %bitcast.11), kind=kLoop, calls=%fused_computation | loop fusion | flops 393216 | bytes 393216 | tf_op jit(solution)/shard_map/concatenate | solution.py:339
  2.5 56.0 %shard_map.91 = bf16[8,64,128]{2,1,0:T(8,128)(2,1)} custom-call(s32[2]{0:T(128)} %len_ref.1, bf16[8,2,48,128]{3,2,1,0:T(8,128)(2,1)} %pad_maximum_fusion.query_ref, bf16[2,4,1024]{2,1,0:T(4,128)(2,1)} %step_key_ref.1, bf16[2,4,1024]{2,1,0:T(4,128)(2,1)} %step_value_ref.1, bf16[2,1024,1024]{2,1,0:T(8,128)(2,1)} %sample_keys.1, ...), custom_call_target="tpu_custom_call" | custom-call | tf_op jit(solution)/shard_map/pallas_call | solution.py:344
  58.5 0.9 %copy.11 = bf16[2,4,8,8,128]{4,3,2,1,0:T(8,128)(2,1)S(1)} copy(bf16[2,4,8,8,128]{4,3,1,0,2:T(8,128)(2,1)} %bitcast.10) | data formatting | bytes 262144 | tf_op jit(solution)/shard_map/transpose | solution.py:387
  59.4 0.7 %reshape.16 = bf16[2,4,8192]{2,1,0:T(4,128)(2,1)} reshape(bf16[2,4,8,8,128]{4,3,2,1,0:T(8,128)(2,1)S(1)} %copy.11) | data formatting | bytes 262144 | tf_op jit(solution)/shard_map/reshape | solution.py:387
  (1 shorter events, 0.0 us)
where the time goes:
time: 60.4 us; the launch traced here: 60.1 us
  Pallas kernels  56 us (93%)
  local copies, waits for them, and re-layouts  2.78 us (5%)
  other arithmetic  1.34 us (2%)
    pallas_call x1, Pallas kernels, body(): pl.pallas_call(functools.partial(kernel, n), out_shape=jax.ShapeDtypeStru...  56 us

commit v1 on v0

v1 whole, which is shorter than its diff:
```python
import functools

import jax
import jax.numpy as jnp
from jax import lax
from jax.experimental import pallas as pl
from jax.experimental.pallas import tpu as pltpu
from jax.sharding import PartitionSpec as P

QUERY_HEADS = 64
KEY_VALUE_HEADS = 8
HEAD_SIZE = 128
HALF = KEY_VALUE_HEADS // 2
GROUP = QUERY_HEADS // KEY_VALUE_HEADS
LOG2E = 1.4426950408889634
FACTOR = (HEAD_SIZE ** (-0.5)) * LOG2E
ID_ROWS = 16
LEVELS = 32767.0
MESH = pl.DeviceIdType.MESH
NT = (((1,), (1,)), ((), ()))
NN = (((1,), (0,)), ((), ()))
F32, BF16, I16 = jnp.float32, jnp.bfloat16, jnp.int16


def quantize(values):
    scale = jnp.maximum(jnp.max(jnp.abs(values), axis=0, keepdims=True), 1e-30)
    return jnp.round(values * (LEVELS / scale)).astype(jnp.int32).astype(I16), scale


def kernel(
    n,
    len_ref,
    id_ref,
    query_ref,
    step_key_ref,
    step_value_ref,
    sample_keys,
    sample_values,
    document_keys,
    document_values,
    out_ref,
    key_buf,
    value_buf,
    doc_keys,
    doc_values,
    value_t,
    query_msg,
    query_pair,
    query_buf,
    own_part,
    own_stat,
    y_send,
    y_send_stat,
    y_got,
    y_got_stat,
    z_send,
    z_send_stat,
    z_got,
    z_got_stat,
    suffix_out,
    suffix_max,
    suffix_total,
    local_sem,
    doc_send,
    doc_recv,
    query_send,
    query_recv,
    y_send_sem,
    y_stat_sem,
    y_recv,
    y_stat_recv,
    z_send_sem,
    z_stat_sem,
    z_recv,
    z_stat_recv,
):
    me = lax.axis_index("seq")
    core = lax.rem(me, 2)
    row = lax.rem(lax.div(me, 2), 2)
    line = lax.div(me, 4)
    lines = n // 4
    samples, cache = sample_keys.shape[0], sample_keys.shape[1]
    steps = step_key_ref.shape[1]
    rows = steps * GROUP
    core_rows = samples * rows
    chip_rows = 2 * core_rows
    prompts, block = document_keys.shape[:2]
    half_width = HALF * HEAD_SIZE
    padded = key_buf.shape[1]

    def device(at_line, at_row, at_core):
        return at_line * 4 + at_row * 2 + at_core

    def line_at(step):
        return lax.rem(line + step, lines)

    def remote(source, target, send, recv, other):
        return pltpu.make_async_remote_copy(
            src_ref=source,
            dst_ref=target,
            send_sem=send,
            recv_sem=recv,
            device_id={"seq": other},
            device_id_type=MESH,
        )

    def arrived(ref, sem):
        pltpu.make_async_copy(ref, ref, sem).wait()

    partner = device(line, row, 1 - core)
    across = device(line, 1 - row, core)

    barrier = pltpu.get_barrier_semaphore()

    def greet(other):
        pl.semaphore_signal(barrier, inc=1, device_id={"seq": other}, device_id_type=MESH)

    greet(partner)
    for c in range(2):
        greet(device(line, 1 - row, c))

    def greet_line(step, carry):
        for c in range(2):
            greet(device(line_at(step), row, c))
        return carry

    lax.fori_loop(1, lines, greet_line, 0)

    def half_of(ref, half):
        return ref.at[:, :, pl.ds(pl.multiple_of(half * half_width, half_width), half_width)]

    def own_rows(ref):
        return ref.at[:, pl.ds(pl.multiple_of(core * block, block), block), :]

    local = [
        pltpu.make_async_copy(half_of(document_keys, core), own_rows(doc_keys), local_sem.at[0]),
        pltpu.make_async_copy(half_of(document_values, core), own_rows(doc_values), local_sem.at[1]),
        pltpu.make_async_copy(sample_keys, key_buf.at[:, pl.ds(0, cache), :], local_sem.at[2]),
        pltpu.make_async_copy(sample_values, value_buf.at[:, pl.ds(0, cache), :], local_sem.at[3]),
    ]
    for copy in local:
        copy.start()

    query_pair[...] = jnp.zeros(query_pair.shape, BF16)
    for s in range(samples):
        for g in range(KEY_VALUE_HEADS):
            first = g * GROUP
            part = jnp.concatenate(
                [
                    query_ref[s, :, (first + r) * HEAD_SIZE : (first + r + 1) * HEAD_SIZE].astype(F32)
                    for r in range(GROUP)
                ],
                axis=0,
            ).astype(BF16)
            query_msg[g // HALF, pl.ds((g % HALF) * core_rows + s * rows, rows), :] = part
            side = g % 2
            query_pair[
                g // 2, s, pl.ds(side * rows, rows), pl.ds(side * HEAD_SIZE, HEAD_SIZE)
            ] = part
    tile_row = lax.broadcasted_iota(jnp.int32, (ID_ROWS, HEAD_SIZE), 0)
    tile_lane = lax.broadcasted_iota(jnp.int32, (ID_ROWS, HEAD_SIZE), 1)
    tile_sample = lax.rem(tile_lane, core_rows) // rows
    marks = jnp.zeros((ID_ROWS, HEAD_SIZE), F32)
    for s in range(samples):
        mine = (tile_row == s) | ((tile_row >= samples) & (tile_sample == s))
        marks = jnp.where(mine, id_ref[s].astype(F32), marks)
    for half in range(2):
        query_msg[half, pl.ds(HALF * core_rows, ID_ROWS), :] = marks.astype(BF16)

    pl.semaphore_wait(barrier, 2 * lines + 1)

    def send_query(half, other):
        remote(query_msg.at[half], query_buf.at[me], query_send, query_recv.at[me], other).start()

    for c in range(2):
        send_query(c, device(line, 1 - row, c))

    def send_line(step, carry):
        target = lax.rem(line + lines - step, lines)
        for c in range(2):
            send_query(c, device(target, row, c))
        return carry

    lax.fori_loop(1, lines, send_line, 0)
    send_query(1 - core, partner)
    swaps = [
        remote(half_of(source, 1 - core), own_rows(target), doc_send.at[k], doc_recv.at[k], partner)
        for k, (source, target) in enumerate(
            ((document_keys, doc_keys), (document_values, doc_values))
        )
    ]
    for copy in swaps:
        copy.start()

    query_buf[me] = query_msg[core]
    for s in range(samples):
        for buf, step_ref in ((key_buf, step_key_ref), (value_buf, step_value_ref)):
            buf[s, pl.ds(cache, padded - cache), :] = jnp.zeros(
                (padded - cache, buf.shape[2]), buf.dtype
            )
            buf[s, pl.ds(cache, steps), :] = step_ref[s]
    local[2].wait()
    local[3].wait()

    slot = lax.broadcasted_iota(jnp.int32, (2 * rows, padded), 1)
    now = lax.rem(lax.broadcasted_iota(jnp.int32, (2 * rows, padded), 0), steps)
    fresh = (slot >= cache) & (slot - cache <= now)

    def suffix(pair, carry=0):
        wide = pl.ds(pl.multiple_of(pair * 2 * HEAD_SIZE, 2 * HEAD_SIZE), 2 * HEAD_SIZE)
        for s in range(samples):
            scores = lax.dot_general(
                query_pair[pair, s], key_buf[s, :, wide], NT, preferred_element_type=F32
            )
            scores = jnp.where((slot < len_ref[s]) | fresh, scores, -jnp.inf)
            peak = jnp.max(scores, axis=1, keepdims=True)
            expo = jnp.exp2((scores - peak) * FACTOR)
            total = jnp.sum(expo, axis=1, keepdims=True)
            result = lax.dot_general(
                expo.astype(BF16), value_buf[s, :, wide], NN, preferred_element_type=F32
            )
            for side in range(2):
                part = pl.ds(side * core_rows + s * rows, rows)
                cut = slice(side * rows, (side + 1) * rows)
                suffix_max[pair, part, :] = peak[cut]
                suffix_total[pair, part, :] = total[cut]
                suffix_out[pair, part, :] = result[
                    cut, side * HEAD_SIZE : (side + 1) * HEAD_SIZE
                ]
        return carry

    lax.fori_loop(0, HALF // 2, suffix, 0)

    local[0].wait()
    local[1].wait()
    for copy in swaps:
        copy.wait_recv()
    for h in range(HALF):
        for p in range(prompts):
            value_t[h, pl.ds(p * HEAD_SIZE, HEAD_SIZE), :] = doc_values[
                p, :, h * HEAD_SIZE : (h + 1) * HEAD_SIZE
            ].T

    lane = lax.broadcasted_iota(jnp.int32, (1, chip_rows), 1)

    def relay(step):
        for c in range(2):
            source = device(line_at(step), row, c)
            arrived(query_buf.at[source], query_recv.at[source])
            remote(
                query_buf.at[source],
                query_buf.at[source],
                query_send,
                query_recv.at[source],
                across,
            ).start()

    def attend(step):
        there = line_at(step)
        mine = [device(there, row, c) for c in range(2)]
        theirs = [device(there, 1 - row, c) for c in range(2)]

        @pl.when(step == 0)
        def _():
            arrived(query_buf.at[partner], query_recv.at[partner])

        for source in theirs:
            arrived(query_buf.at[source], query_recv.at[source])
        sources = mine + theirs
        tiles = [
            query_buf[source, pl.ds(HALF * core_rows, ID_ROWS), :].astype(F32)
            for source in sources
        ]
        masks = [
            jnp.concatenate(
                [
                    jnp.broadcast_to(
                        jnp.where(tile[s : s + 1] == p, 1.0, 0.0), (rows, HEAD_SIZE)
                    )
                    for tile in tiles
                    for s in range(samples)
                ],
                axis=0,
            ).astype(BF16)
            for p in range(prompts)
        ]
        marks = jnp.concatenate(
            [
                jnp.where(
                    lane < core_rows,
                    tiles[2 * k][samples : samples + 1],
                    tiles[2 * k + 1][samples : samples + 1],
                )
                for k in range(2)
            ],
            axis=1,
        )
        for pair in range(HALF // 2):
            stats = []
            for h in (2 * pair, 2 * pair + 1):
                query = jnp.concatenate(
                    [query_buf[source, pl.ds(h * core_rows, core_rows), :] for source in sources],
                    axis=0,
                )
                query = jnp.concatenate([query * mask for mask in masks], axis=1)
                cols = slice(h * HEAD_SIZE, (h + 1) * HEAD_SIZE)
                keys = jnp.concatenate([doc_keys[p, :, cols] for p in range(prompts)], axis=1)
                scores = lax.dot_general(keys, query, NT, preferred_element_type=F32)
                peak = jnp.max(scores, axis=0, keepdims=True)
                expo = jnp.exp2((scores - peak) * FACTOR)
                total = jnp.sum(expo, axis=0, keepdims=True)
                both = lax.dot_general(
                    value_t[h], expo.astype(BF16), NN, preferred_element_type=F32
                )
                result = both[:HEAD_SIZE]
                for p in range(1, prompts):
                    result = jnp.where(
                        marks == p, both[p * HEAD_SIZE : (p + 1) * HEAD_SIZE], result
                    )
                own_part[step, h] = result[:, :chip_rows]
                own_stat[step, h, 0:1, :] = peak[:, :chip_rows]
                own_stat[step, h, 1:2, :] = total[:, :chip_rows]
                y_send[step, h], scale = quantize(result[:, chip_rows:])
                stats += [peak[:, chip_rows:], total[:, chip_rows:], scale]
            y_send_stat[step, pair] = jnp.concatenate(
                stats + [jnp.zeros((2, chip_rows), F32)], axis=0
            )
            heads = pl.ds(2 * pair, 2)
            remote(
                y_send.at[step, heads],
                y_got.at[step, heads],
                y_send_sem,
                y_recv.at[step, pair],
                across,
            ).start()
            remote(
                y_send_stat.at[step, pair],
                y_got_stat.at[step, pair],
                y_stat_sem,
                y_stat_recv.at[step, pair],
                across,
            ).start()

    def give(source, target, send, recv, other):
        @pl.when(other != me)
        def _():
            remote(source, target, send, recv, other).start()

        @pl.when(other == me)
        def _():
            pltpu.make_async_copy(source, target, recv).start()

    def combine(step):
        there = line_at(step)
        stats = [[], []]
        for pair in range(HALF // 2):
            arrived(y_got.at[step, pl.ds(2 * pair, 2)], y_recv.at[step, pair])
            arrived(y_got_stat.at[step, pair], y_stat_recv.at[step, pair])
            merged = []
            got = y_got_stat[step, pair]
            for side in range(2):
                h = 2 * pair + side
                peak_a, total_a = own_stat[step, h, 0:1, :], own_stat[step, h, 1:2, :]
                peak_b, total_b, scale_b = (
                    got[3 * side : 3 * side + 1],
                    got[3 * side + 1 : 3 * side + 2],
                    got[3 * side + 2 : 3 * side + 3],
                )
                top = jnp.maximum(peak_a, peak_b)
                weight_a = jnp.exp2((peak_a - top) * FACTOR)
                weight_b = jnp.exp2((peak_b - top) * FACTOR)
                result = own_part[step, h] * weight_a + y_got[step, h].astype(jnp.int32).astype(
                    F32
                ) * (weight_b * (scale_b * (1.0 / LEVELS)))
                merged.append((result, top, total_a * weight_a + total_b * weight_b))
            for c in range(2):
                mixed = []
                for low, high in zip(*merged):
                    wide = jnp.broadcast_to(low, (max(8, low.shape[0]), chip_rows))
                    wide_high = jnp.broadcast_to(high, wide.shape)
                    if c == 0:
                        wide_high = pltpu.roll(wide_high, core_rows, 1)
                    else:
                        wide = pltpu.roll(wide, core_rows, 1)
                    mixed.append(
                        jnp.where(lane < core_rows, wide, wide_high)[: low.shape[0]]
                    )
                result, top, total = mixed
                at = (step * 2 + c) * 2 + pair
                z_send[at], scale = quantize(result)
                stats[c] += [top, total, scale]
                give(
                    z_send.at[at],
                    z_got.at[step, core, pair],
                    z_send_sem,
                    z_recv.at[step, core, pair],
                    device(there, row, c),
                )
        for c in range(2):
            z_send_stat[step * 2 + c] = jnp.concatenate(
                stats[c] + [jnp.zeros((2, chip_rows), F32)], axis=0
            )
            give(
                z_send_stat.at[step * 2 + c],
                z_got_stat.at[step, core],
                z_stat_sem,
                z_stat_recv.at[step, core],
                device(there, row, c),
            )

    def advance(step, carry):
        @pl.when(step + 1 < lines)
        def _():
            relay(step + 1)

        attend(step)

        @pl.when(step >= 1)
        def _():
            combine(step - 1)

        return carry

    lax.fori_loop(0, lines, advance, 0)
    suffix(HALF // 2)
    combine(lines - 1)
    lax.fori_loop(HALF // 2 + 1, HALF, suffix, 0)

    for half in range(2):
        for step in range(lines):
            arrived(z_got_stat.at[step, half], z_stat_recv.at[step, half])
        for pair in range(HALF // 2):
            for step in range(lines):
                arrived(z_got.at[step, half, pair], z_recv.at[step, half, pair])
            tops = [z_got_stat[step, half, 3 * pair : 3 * pair + 1, :] for step in range(lines)]
            top = functools.reduce(jnp.maximum, tops)
            above, below = 0.0, 0.0
            for step in range(lines):
                weight = jnp.exp2((tops[step] - top) * FACTOR)
                below = below + z_got_stat[step, half, 3 * pair + 1 : 3 * pair + 2, :] * weight
                scale = z_got_stat[step, half, 3 * pair + 2 : 3 * pair + 3, :]
                above = above + z_got[step, half, pair].astype(jnp.int32).astype(F32) * (
                    weight * (scale * (1.0 / LEVELS))
                )
            turned = jnp.concatenate([top, below, jnp.zeros((6, chip_rows), F32)], axis=0).T
            peak, total = turned[:, 0:1], turned[:, 1:2]
            at = half * (HALF // 2) + pair
            top = jnp.maximum(peak, suffix_max[at])
            weight = jnp.exp2((peak - top) * FACTOR)
            weight_own = jnp.exp2((suffix_max[at] - top) * FACTOR)
            out_ref[at] = (
                (above.T * weight + suffix_out[at] * weight_own)
                / (total * weight + suffix_total[at] * weight_own)
            ).astype(out_ref.dtype)

    sent = query_buf.at[pl.ds(0, n - 1)]
    pltpu.make_async_copy(sent, sent, query_send).wait()
    pltpu.make_async_copy(y_send, y_send, y_send_sem).wait()
    pltpu.make_async_copy(y_send_stat, y_send_stat, y_stat_sem).wait()
    sent = z_send.at[pl.ds(0, 4 * lines - 2)]
    pltpu.make_async_copy(sent, sent, z_send_sem).wait()
    sent = z_send_stat.at[pl.ds(0, 2 * lines - 1)]
    pltpu.make_async_copy(sent, sent, z_stat_sem).wait()
    for copy in swaps:
        copy.wait_send()


def body(
    queries,
    step_keys,
    step_values,
    sample_keys,
    sample_values,
    suffix_len,
    prompt_id,
    document_keys,
    document_values,
):
    n = lax.axis_size("seq")
    samples, steps = queries.shape[:2]
    cache = sample_keys.shape[1]
    width = KEY_VALUE_HEADS * HEAD_SIZE
    half_width = HALF * HEAD_SIZE
    prompts, block = document_keys.shape[:2]
    rows = steps * GROUP
    core_rows = samples * rows
    chip_rows = 2 * core_rows
    lines = n // 4
    padded = cache + 128
    pairs = HALF // 2
    vmem = pl.BlockSpec(memory_space=pltpu.VMEM)
    smem = pl.BlockSpec(memory_space=pltpu.SMEM)
    hbm = pl.BlockSpec(memory_space=pl.ANY)
    dma = pltpu.SemaphoreType.DMA
    result = pl.pallas_call(
        functools.partial(kernel, n),
        out_shape=jax.ShapeDtypeStruct((2 * pairs, 2 * core_rows, HEAD_SIZE), BF16),
        in_specs=[smem, smem, vmem, vmem, vmem, hbm, hbm, hbm, hbm],
        out_specs=vmem,
        scratch_shapes=[
            pltpu.VMEM((samples, padded, width), BF16),
            pltpu.VMEM((samples, padded, width), BF16),
            pltpu.VMEM((prompts, 2 * block, half_width), BF16),
            pltpu.VMEM((prompts, 2 * block, half_width), BF16),
            pltpu.VMEM((HALF, prompts * HEAD_SIZE, 2 * block), BF16),
            pltpu.VMEM((2, HALF * core_rows + ID_ROWS, HEAD_SIZE), BF16),
            pltpu.VMEM((2 * pairs, samples, 2 * rows, 2 * HEAD_SIZE), BF16),
            pltpu.VMEM((n, HALF * core_rows + ID_ROWS, HEAD_SIZE), BF16),
            pltpu.VMEM((lines, HALF, HEAD_SIZE, chip_rows), F32),
            pltpu.VMEM((lines, HALF, 8, chip_rows), F32),
            pltpu.VMEM((lines, HALF, HEAD_SIZE, chip_rows), I16),
            pltpu.VMEM((lines, pairs, 8, chip_rows), F32),
            pltpu.VMEM((lines, HALF, HEAD_SIZE, chip_rows), I16),
            pltpu.VMEM((lines, pairs, 8, chip_rows), F32),
            pltpu.VMEM((lines * 2 * pairs, HEAD_SIZE, chip_rows), I16),
            pltpu.VMEM((lines * 2, 8, chip_rows), F32),
            pltpu.VMEM((lines, 2, pairs, HEAD_SIZE, chip_rows), I16),
            pltpu.VMEM((lines, 2, 8, chip_rows), F32),
            pltpu.VMEM((2 * pairs, 2 * core_rows, HEAD_SIZE), F32),
            pltpu.VMEM((2 * pairs, 2 * core_rows, 1), F32),
            pltpu.VMEM((2 * pairs, 2 * core_rows, 1), F32),
            dma((4,)),
            dma((2,)),
            dma((2,)),
            dma,
            dma((n,)),
            dma,
            dma,
            dma((lines, pairs)),
            dma((lines, pairs)),
            dma,
            dma,
            dma((lines, 2, pairs)),
            dma((lines, 2)),
        ],
        compiler_params=pltpu.CompilerParams(
            collective_id=0, has_side_effects=True, vmem_limit_bytes=60 << 20
        ),
    )(
        suffix_len,
        prompt_id,
        queries,
        step_keys,
        step_values,
        sample_keys,
        sample_values,
        document_keys,
        document_values,
    )
    result = result.reshape(KEY_VALUE_HEADS, samples, GROUP, steps, HEAD_SIZE)
    return result.transpose(1, 3, 0, 2, 4).reshape(samples, steps, QUERY_HEADS * HEAD_SIZE)


def solution(mesh):
    return jax.shard_map(
        body,
        mesh=mesh,
        in_specs=(
            P(("groups", "seq"), None, None),
            P(("groups", "seq"), None, None),
            P(("groups", "seq"), None, None),
            P(("groups", "seq"), None, None),
            P(("groups", "seq"), None, None),
            P(("groups", "seq")),
            P(("groups", "seq")),
            P("groups", "seq", None),
            P("groups", "seq", None),
        ),
        out_specs=P(("groups", "seq"), None, None),
        check_vma=False,
    )
```

time: 60.4 us -> 44.1 us (0.73)
  the two profiles are of different devices: /device:TPU:0 before, /device:TPU:25 now
where the time goes in v1:
time: 44.1 us; the launch traced here: 43.9 us
  Pallas kernels  42.3 us (96%)
  local copies, waits for them, and re-layouts  1.62 us (4%)
    pallas_call x1, Pallas kernels, body(): pl.pallas_call(functools.partial(kernel, n), out_shape=jax.ShapeDtypeStru...  42.3 us
    transpose x1, local copies, waits for them, and re-layouts, body(): result.transpose(1, 3, 0, 2, 4)  0.92 us

profile of v1, /device:TPU:25, one launch (start us, length us, event | category | flops | bytes accessed | tf_op | source)
XLA Modules:
  0.0 43.9 jit_solution(6138813825236378962)
XLA Ops:
  0.0 42.3 %shard_map.91 = bf16[4,128,128]{2,1,0:T(8,128)(2,1)} custom-call(s32[2]{0:T(128)} %len_ref.1, s32[2]{0:T(128)} %id_ref.1, bf16[2,4,8192]{2,1,0:T(4,128)(2,1)} %query_ref.1, bf16[2,4,1024]{2,1,0:T(4,128)(2,1)} %step_key_ref.1, bf16[2,4,1024]{2,1,0:T(4,128)(2,1)} %step_value_ref.1, bf16[2,1024,1024]{2,1,0:T(8,128)(2,1)} %sample_keys.1, ...), custom_call_target="tpu_custom_call" | custom-call | tf_op jit(solution)/shard_map/pallas_call | solution.py:495
  42.3 0.9 %copy.10 = bf16[2,4,8,8,128]{4,3,2,1,0:T(8,128)(2,1)S(1)} copy(bf16[2,4,8,8,128]{4,1,3,0,2:T(4,128)(2,1)} %bitcast.5) | data formatting | bytes 262144 | tf_op jit(solution)/shard_map/transpose | solution.py:551
  43.2 0.7 %reshape.7 = bf16[2,4,8192]{2,1,0:T(4,128)(2,1)} reshape(bf16[2,4,8,8,128]{4,3,2,1,0:T(8,128)(2,1)S(1)} %copy.10) | data formatting | bytes 262144 | tf_op jit(solution)/shard_map/reshape | solution.py:551

commit v2 on v1

--- a/solution.py
+++ b/solution.py
@@ -31,14 +31,17 @@
     n,
     len_ref,
     id_ref,
-    query_ref,
-    step_key_ref,
-    step_value_ref,
+    queries,
+    step_keys,
+    step_values,
     sample_keys,
     sample_values,
     document_keys,
     document_values,
     out_ref,
+    query_ref,
+    step_key_ref,
+    step_value_ref,
     key_buf,
     value_buf,
     doc_keys,
@@ -80,7 +83,7 @@
     line = lax.div(me, 4)
     lines = n // 4
     samples, cache = sample_keys.shape[0], sample_keys.shape[1]
-    steps = step_key_ref.shape[1]
+    steps = step_keys.shape[1]
     rows = steps * GROUP
     core_rows = samples * rows
     chip_rows = 2 * core_rows
@@ -132,15 +135,21 @@
     def own_rows(ref):
         return ref.at[:, pl.ds(pl.multiple_of(core * block, block), block), :]
 
+    small = [
+        pltpu.make_async_copy(queries, query_ref, local_sem.at[4]),
+        pltpu.make_async_copy(step_keys, step_key_ref, local_sem.at[5]),
+        pltpu.make_async_copy(step_values, step_value_ref, local_sem.at[6]),
+    ]
     local = [
         pltpu.make_async_copy(half_of(document_keys, core), own_rows(doc_keys), local_sem.at[0]),
         pltpu.make_async_copy(half_of(document_values, core), own_rows(doc_values), local_sem.at[1]),
         pltpu.make_async_copy(sample_keys, key_buf.at[:, pl.ds(0, cache), :], local_sem.at[2]),
         pltpu.make_async_copy(sample_values, value_buf.at[:, pl.ds(0, cache), :], local_sem.at[3]),
     ]
-    for copy in local:
+    for copy in small + local:
         copy.start()
 
+    small[0].wait()
     query_pair[...] = jnp.zeros(query_pair.shape, BF16)
     for s in range(samples):
         for g in range(KEY_VALUE_HEADS):
@@ -193,6 +202,8 @@
         copy.start()
 
     query_buf[me] = query_msg[core]
+    small[1].wait()
+    small[2].wait()
     for s in range(samples):
         for buf, step_ref in ((key_buf, step_key_ref), (value_buf, step_value_ref)):
             buf[s, pl.ds(cache, padded - cache), :] = jnp.zeros(
@@ -413,6 +424,10 @@
         def _():
             relay(step + 1)
 
+        @pl.when((step >= HALF // 2) & (step < HALF))
+        def _():
+            suffix(step)
+
         attend(step)
 
         @pl.when(step >= 1)
@@ -422,9 +437,8 @@
         return carry
 
     lax.fori_loop(0, lines, advance, 0)
-    suffix(HALF // 2)
     combine(lines - 1)
-    lax.fori_loop(HALF // 2 + 1, HALF, suffix, 0)
+    lax.fori_loop(min(lines, HALF), HALF, suffix, 0)
 
     for half in range(2):
         for step in range(lines):
@@ -448,10 +462,17 @@
             top = jnp.maximum(peak, suffix_max[at])
             weight = jnp.exp2((peak - top) * FACTOR)
             weight_own = jnp.exp2((suffix_max[at] - top) * FACTOR)
-            out_ref[at] = (
-                (above.T * weight + suffix_out[at] * weight_own)
-                / (total * weight + suffix_total[at] * weight_own)
-            ).astype(out_ref.dtype)
+            result = (above.T * weight + suffix_out[at] * weight_own) / (
+                total * weight + suffix_total[at] * weight_own
+            )
+            for side in range(2):
+                for s in range(samples):
+                    for r in range(GROUP):
+                        first = side * core_rows + s * rows + r * steps
+                        head = (2 * at + side) * GROUP + r
+                        out_ref[s, :, head * HEAD_SIZE : (head + 1) * HEAD_SIZE] = result[
+                            first : first + steps
+                        ].astype(out_ref.dtype)
 
     sent = query_buf.at[pl.ds(0, n - 1)]
     pltpu.make_async_copy(sent, sent, query_send).wait()
@@ -492,12 +513,15 @@
     smem = pl.BlockSpec(memory_space=pltpu.SMEM)
     hbm = pl.BlockSpec(memory_space=pl.ANY)
     dma = pltpu.SemaphoreType.DMA
-    result = pl.pallas_call(
+    return pl.pallas_call(
         functools.partial(kernel, n),
-        out_shape=jax.ShapeDtypeStruct((2 * pairs, 2 * core_rows, HEAD_SIZE), BF16),
-        in_specs=[smem, smem, vmem, vmem, vmem, hbm, hbm, hbm, hbm],
+        out_shape=jax.ShapeDtypeStruct(queries.shape, BF16),
+        in_specs=[smem, smem, hbm, hbm, hbm, hbm, hbm, hbm, hbm],
         out_specs=vmem,
         scratch_shapes=[
+            pltpu.VMEM(queries.shape, BF16),
+            pltpu.VMEM(step_keys.shape, BF16),
+            pltpu.VMEM(step_values.shape, BF16),
             pltpu.VMEM((samples, padded, width), BF16),
             pltpu.VMEM((samples, padded, width), BF16),
             pltpu.VMEM((prompts, 2 * block, half_width), BF16),
@@ -519,7 +543,7 @@
             pltpu.VMEM((2 * pairs, 2 * core_rows, HEAD_SIZE), F32),
             pltpu.VMEM((2 * pairs, 2 * core_rows, 1), F32),
             pltpu.VMEM((2 * pairs, 2 * core_rows, 1), F32),
-            dma((4,)),
+            dma((7,)),
             dma((2,)),
             dma((2,)),
             dma,
@@ -547,8 +571,6 @@
         document_keys,
         document_values,
     )
-    result = result.reshape(KEY_VALUE_HEADS, samples, GROUP, steps, HEAD_SIZE)
-    return result.transpose(1, 3, 0, 2, 4).reshape(samples, steps, QUERY_HEADS * HEAD_SIZE)
 
 
 def solution(mesh):

time: 44.1 us -> 43.8 us (level)
  the two profiles are of different devices: /device:TPU:25 before, /device:TPU:0 now
where the time goes in v2:
time: 43.8 us; the launch traced here: 43.2 us
  Pallas kernels  41.6 us (95%)
  local copies, waits for them, and re-layouts  1.61 us (4%)
    pallas_call x1, Pallas kernels, body(): pl.pallas_call(functools.partial(kernel, n), out_shape=jax.ShapeDtypeStru...  41.6 us
    unnamed x1, local copies, waits for them, and re-layouts  1.61 us

profile of v2, /device:TPU:0, one launch (start us, length us, event | category | flops | bytes accessed | tf_op | source)
XLA Modules:
  0.0 43.2 jit_solution(9944545661889612751)
XLA Ops:
  0.0 41.6 %shard_map.91 = bf16[2,4,8192]{2,1,0:T(4,128)(2,1)} custom-call(s32[2]{0:T(128)} %len_ref.1, s32[2]{0:T(128)} %id_ref.1, bf16[2,4,8192]{2,1,0:T(4,128)(2,1)} %queries.1, bf16[2,4,1024]{2,1,0:T(4,128)(2,1)} %step_keys.1, bf16[2,4,1024]{2,1,0:T(4,128)(2,1)} %step_values.1, bf16[2,1024,1024]{2,1,0:T(8,128)(2,1)} %sample_keys.1, ...), custom_call_target="tpu_custom_call" | custom-call | tf_op jit(solution)/shard_map/pallas_call | solution.py:516
  41.6 1.6 %copy.11 = bf16[2,4,8192]{2,1,0:T(4,128)(2,1)} copy(bf16[2,4,8192]{2,1,0:T(4,128)(2,1)} %shard_map.91) | data formatting | bytes 262144

commit v3 on v2

--- a/solution.py
+++ b/solution.py
@@ -29,8 +29,8 @@
 
 def kernel(
     n,
-    len_ref,
-    id_ref,
+    lengths,
+    prompt_id,
     queries,
     step_keys,
     step_values,
@@ -39,6 +39,8 @@
     document_keys,
     document_values,
     out_ref,
+    len_ref,
+    id_ref,
     query_ref,
     step_key_ref,
     step_value_ref,
@@ -139,6 +141,8 @@
         pltpu.make_async_copy(queries, query_ref, local_sem.at[4]),
         pltpu.make_async_copy(step_keys, step_key_ref, local_sem.at[5]),
         pltpu.make_async_copy(step_values, step_value_ref, local_sem.at[6]),
+        pltpu.make_async_copy(prompt_id, id_ref, local_sem.at[7]),
+        pltpu.make_async_copy(lengths, len_ref, local_sem.at[8]),
     ]
     local = [
         pltpu.make_async_copy(half_of(document_keys, core), own_rows(doc_keys), local_sem.at[0]),
@@ -166,6 +170,7 @@
             query_pair[
                 g // 2, s, pl.ds(side * rows, rows), pl.ds(side * HEAD_SIZE, HEAD_SIZE)
             ] = part
+    small[3].wait()
     tile_row = lax.broadcasted_iota(jnp.int32, (ID_ROWS, HEAD_SIZE), 0)
     tile_lane = lax.broadcasted_iota(jnp.int32, (ID_ROWS, HEAD_SIZE), 1)
     tile_sample = lax.rem(tile_lane, core_rows) // rows
@@ -204,6 +209,7 @@
     query_buf[me] = query_msg[core]
     small[1].wait()
     small[2].wait()
+    small[4].wait()
     for s in range(samples):
         for buf, step_ref in ((key_buf, step_key_ref), (value_buf, step_value_ref)):
             buf[s, pl.ds(cache, padded - cache), :] = jnp.zeros(
@@ -467,12 +473,11 @@
             )
             for side in range(2):
                 for s in range(samples):
-                    for r in range(GROUP):
-                        first = side * core_rows + s * rows + r * steps
-                        head = (2 * at + side) * GROUP + r
-                        out_ref[s, :, head * HEAD_SIZE : (head + 1) * HEAD_SIZE] = result[
-                            first : first + steps
-                        ].astype(out_ref.dtype)
+                    first = side * core_rows + s * rows
+                    target = (s * KEY_VALUE_HEADS + 2 * at + side) * rows
+                    out_ref[pl.ds(target, rows), :] = result[first : first + rows].astype(
+                        out_ref.dtype
+                    )
 
     sent = query_buf.at[pl.ds(0, n - 1)]
     pltpu.make_async_copy(sent, sent, query_send).wait()
@@ -510,15 +515,16 @@
     padded = cache + 128
     pairs = HALF // 2
     vmem = pl.BlockSpec(memory_space=pltpu.VMEM)
-    smem = pl.BlockSpec(memory_space=pltpu.SMEM)
     hbm = pl.BlockSpec(memory_space=pl.ANY)
     dma = pltpu.SemaphoreType.DMA
-    return pl.pallas_call(
+    result = pl.pallas_call(
         functools.partial(kernel, n),
-        out_shape=jax.ShapeDtypeStruct(queries.shape, BF16),
-        in_specs=[smem, smem, hbm, hbm, hbm, hbm, hbm, hbm, hbm],
+        out_shape=pltpu.VMEM((samples * QUERY_HEADS * steps, HEAD_SIZE), BF16),
+        in_specs=[hbm, hbm, hbm, hbm, hbm, hbm, hbm, hbm, hbm],
         out_specs=vmem,
         scratch_shapes=[
+            pltpu.SMEM(suffix_len.shape, jnp.int32),
+            pltpu.SMEM(prompt_id.shape, jnp.int32),
             pltpu.VMEM(queries.shape, BF16),
             pltpu.VMEM(step_keys.shape, BF16),
             pltpu.VMEM(step_values.shape, BF16),
@@ -543,7 +549,7 @@
             pltpu.VMEM((2 * pairs, 2 * core_rows, HEAD_SIZE), F32),
             pltpu.VMEM((2 * pairs, 2 * core_rows, 1), F32),
             pltpu.VMEM((2 * pairs, 2 * core_rows, 1), F32),
-            dma((7,)),
+            dma((9,)),
             dma((2,)),
             dma((2,)),
             dma,
@@ -571,6 +577,7 @@
         document_keys,
         document_values,
     )
+    return result.reshape(samples, QUERY_HEADS, steps, HEAD_SIZE).transpose(0, 2, 1, 3).reshape(queries.shape)
 
 
 def solution(mesh):

time: 43.8 us -> 41.4 us (0.945)
  Pallas kernels: 41.6 us -> 40.2 us
  local copies, waits for them, and re-layouts: 1.61 us -> 0.66 us
    pallas_call x1, Pallas kernels: 41.6 us -> 40.2 us  [body(): pl.pallas_call(functools.partial(kernel, n), out_shape=pltpu.VMEM((sample...]
    unnamed x1, local copies, waits for them, and re-layouts: 1.61 us -> 0.66 us
where the time goes in v3:
time: 41.4 us; the launch traced here: 40.9 us
  Pallas kernels  40.2 us (97%)
  local copies, waits for them, and re-layouts  0.66 us (2%)
    pallas_call x1, Pallas kernels, body(): pl.pallas_call(functools.partial(kernel, n), out_shape=pltpu.VMEM((sample...  40.2 us

profile of v3, /device:TPU:0, one launch (start us, length us, event | category | flops | bytes accessed | tf_op | source)
XLA Modules:
  0.0 40.9 jit_solution(5306974363278015509)
XLA Ops:
  0.0 40.2 %shard_map.91 = bf16[512,128]{1,0:T(8,128)(2,1)S(1)} custom-call(s32[2]{0:T(128)} %lengths.1, s32[2]{0:T(128)} %prompt_id.1, bf16[2,4,8192]{2,1,0:T(4,128)(2,1)} %queries.1, bf16[2,4,1024]{2,1,0:T(4,128)(2,1)} %step_keys.1, bf16[2,4,1024]{2,1,0:T(4,128)(2,1)} %step_values.1, bf16[2,1024,1024]{2,1,0:T(8,128)(2,1)} %sample_keys.1, ...), custom_call_target="tpu_custom_call" | custom-call | tf_op jit(solution)/shard_map/pallas_call | solution.py:520
  40.2 0.7 %copy.12 = bf16[2,4,8192]{2,1,0:T(4,128)(2,1)} copy(bf16[2,4,8192]{2,1,0:T(4,128)(2,1)S(1)} %bitcast.5) | data formatting | bytes 262144

commit v4 on v3

--- a/solution.py
+++ b/solution.py
@@ -62,6 +62,8 @@
     z_send_stat,
     z_got,
     z_got_stat,
+    sum_part,
+    sum_stat,
     suffix_out,
     suffix_max,
     suffix_total,
@@ -69,6 +71,7 @@
     doc_send,
     doc_recv,
     query_send,
+    forward_sem,
     query_recv,
     y_send_sem,
     y_stat_sem,
@@ -96,8 +99,29 @@
     def device(at_line, at_row, at_core):
         return at_line * 4 + at_row * 2 + at_core
 
+    couples = lines // 2
+    couple, member = lax.div(line, 2), lax.rem(line, 2)
+    mate = line + 1 - 2 * member
+
+    def wraps(turn):
+        return lax.div(couple + turn, couples)
+
+    def couple_at(turn):
+        return couple + turn - wraps(turn) * couples
+
+    def turn_at(step):
+        return lax.div(step, 2)
+
     def line_at(step):
-        return lax.rem(line + step, lines)
+        turn, second = turn_at(step), lax.rem(step, 2)
+        first = wraps(turn) + (1 - jnp.minimum(turn, 1)) * member
+        return couple_at(turn) * 2 + first + second - 2 * first * second
+
+    def gateway(turn):
+        return (turn >= 1) & (member == 1 - wraps(turn))
+
+    inner = gateway(1)
+    upper = wraps(1) == 1
 
     def remote(source, target, send, recv, other):
         return pltpu.make_async_remote_copy(
@@ -126,7 +150,7 @@
 
     def greet_line(step, carry):
         for c in range(2):
-            greet(device(line_at(step), row, c))
+            greet(device(lax.rem(line + step, lines), row, c))
         return carry
 
     lax.fori_loop(1, lines, greet_line, 0)
@@ -189,13 +213,15 @@
     for c in range(2):
         send_query(c, device(line, 1 - row, c))
 
-    def send_line(step, carry):
-        target = lax.rem(line + lines - step, lines)
+    for c in range(2):
+        send_query(c, device(mate, row, c))
+
+    def send_far(turn, carry):
         for c in range(2):
-            send_query(c, device(target, row, c))
+            send_query(c, device(couple_at(turn) * 2 + wraps(turn), row, c))
         return carry
 
-    lax.fori_loop(1, lines, send_line, 0)
+    lax.fori_loop(1, couples, send_far, 0)
     send_query(1 - core, partner)
     swaps = [
         remote(half_of(source, 1 - core), own_rows(target), doc_send.at[k], doc_recv.at[k], partner)
@@ -264,6 +290,18 @@
         for c in range(2):
             source = device(line_at(step), row, c)
             arrived(query_buf.at[source], query_recv.at[source])
+            turn = turn_at(step)
+
+            @pl.when(gateway(turn))
+            def _():
+                remote(
+                    query_buf.at[source],
+                    query_buf.at[source],
+                    forward_sem.at[turn],
+                    query_recv.at[source],
+                    device(mate, row, core),
+                ).start()
+
             remote(
                 query_buf.at[source],
                 query_buf.at[source],
@@ -369,7 +407,7 @@
 
     def combine(step):
         there = line_at(step)
-        stats = [[], []]
+        place = 2 * turn_at(step) + member
         for pair in range(HALF // 2):
             arrived(y_got.at[step, pl.ds(2 * pair, 2)], y_recv.at[step, pair])
             arrived(y_got_stat.at[step, pair], y_stat_recv.at[step, pair])
@@ -405,87 +443,135 @@
                 result, top, total = mixed
                 at = (step * 2 + c) * 2 + pair
                 z_send[at], scale = quantize(result)
-                stats[c] += [top, total, scale]
+                z_send_stat[at, 0:1, :] = top
+                z_send_stat[at, 1:2, :] = total
+                z_send_stat[at, 2:3, :] = scale
                 give(
                     z_send.at[at],
-                    z_got.at[step, core, pair],
+                    z_got.at[place, core, pair],
                     z_send_sem,
-                    z_recv.at[step, core, pair],
+                    z_recv.at[place, core, pair],
                     device(there, row, c),
                 )
-        for c in range(2):
-            z_send_stat[step * 2 + c] = jnp.concatenate(
-                stats[c] + [jnp.zeros((2, chip_rows), F32)], axis=0
-            )
-            give(
-                z_send_stat.at[step * 2 + c],
-                z_got_stat.at[step, core],
-                z_stat_sem,
-                z_stat_recv.at[step, core],
-                device(there, row, c),
-            )
-
-    def advance(step, carry):
-        @pl.when(step + 1 < lines)
-        def _():
-            relay(step + 1)
-
-        @pl.when((step >= HALF // 2) & (step < HALF))
-        def _():
-            suffix(step)
-
-        attend(step)
-
-        @pl.when(step >= 1)
-        def _():
-            combine(step - 1)
+                give(
+                    z_send_stat.at[at],
+                    z_got_stat.at[place, core, pair],
+                    z_stat_sem,
+                    z_stat_recv.at[place, core, pair],
+                    device(there, row, c),
+                )
+
+    def attend_at(trip):
+        outer = jnp.where(upper & (trip >= 2), trip + 1 - 2 * lax.rem(trip, 2), trip + 0)
+        return jnp.where(inner, jnp.where(trip <= lines - 3, trip + 2, trip + 2 - lines), outer)
+
+    def relay_at(index):
+        outer = index + 1
+        return jnp.where(inner, jnp.where(index <= lines - 3, index + 2, 1), outer)
+
+    def advance(trip, carry):
+        @pl.when((trip == 0) == inner)
+        def _():
+            @pl.when(trip <= 1)
+            def _():
+                relay(relay_at(1))
+
+        @pl.when((trip >= 1) & (trip <= HALF // 2))
+        def _():
+            suffix(trip + HALF // 2 - 1)
+
+        index = trip + 1 - jnp.where(inner, 1, 0)
+
+        @pl.when((index >= 2) & (index <= lines - 2))
+        def _():
+            relay(relay_at(index))
+
+        attend(attend_at(trip))
+
+        @pl.when(trip >= 1)
+        def _():
+            combine(attend_at(trip - 1))
 
         return carry
 
+    relay(relay_at(0))
     lax.fori_loop(0, lines, advance, 0)
-    combine(lines - 1)
-    lax.fori_loop(min(lines, HALF), HALF, suffix, 0)
-
-    for half in range(2):
-        for step in range(lines):
-            arrived(z_got_stat.at[step, half], z_stat_recv.at[step, half])
+    combine(attend_at(lines - 1))
+
+    last = jnp.where(inner, 2 + member, 1 - member)
+
+    def gather(place, at, half, pair):
+        arrived(z_got_stat.at[place, half, pair], z_stat_recv.at[place, half, pair])
+        arrived(z_got.at[place, half, pair], z_recv.at[place, half, pair])
+        peak = z_got_stat[place, half, pair, 0:1, :]
+        total = z_got_stat[place, half, pair, 1:2, :]
+        scale = z_got_stat[place, half, pair, 2:3, :]
+        before = sum_stat[at, 0:1, :]
+        top = jnp.maximum(before, peak)
+        old = jnp.exp2((before - top) * FACTOR)
+        new = jnp.exp2((peak - top) * FACTOR)
+        above = sum_part[at] * old + z_got[place, half, pair].astype(jnp.int32).astype(F32) * (
+            new * (scale * (1.0 / LEVELS))
+        )
+        return above, top, sum_stat[at, 1:2, :] * old + total * new
+
+    def tiles(place, use):
         for pair in range(HALF // 2):
-            for step in range(lines):
-                arrived(z_got.at[step, half, pair], z_recv.at[step, half, pair])
-            tops = [z_got_stat[step, half, 3 * pair : 3 * pair + 1, :] for step in range(lines)]
-            top = functools.reduce(jnp.maximum, tops)
-            above, below = 0.0, 0.0
-            for step in range(lines):
-                weight = jnp.exp2((tops[step] - top) * FACTOR)
-                below = below + z_got_stat[step, half, 3 * pair + 1 : 3 * pair + 2, :] * weight
-                scale = z_got_stat[step, half, 3 * pair + 2 : 3 * pair + 3, :]
-                above = above + z_got[step, half, pair].astype(jnp.int32).astype(F32) * (
-                    weight * (scale * (1.0 / LEVELS))
+            for half in range(2):
+                at = half * (HALF // 2) + pair
+                use(at, *gather(place, at, half, pair))
+
+    def keep(at, above, top, total):
+        sum_part[at] = above
+        sum_stat[at, 0:1, :] = top
+        sum_stat[at, 1:2, :] = total
+
+    def finish(at, above, top, total):
+        turned = jnp.concatenate([top, total, jnp.zeros((6, chip_rows), F32)], axis=0).T
+        peak, total = turned[:, 0:1], turned[:, 1:2]
+        top = jnp.maximum(peak, suffix_max[at])
+        weight = jnp.exp2((peak - top) * FACTOR)
+        weight_own = jnp.exp2((suffix_max[at] - top) * FACTOR)
+        result = (above.T * weight + suffix_out[at] * weight_own) / (
+            total * weight + suffix_total[at] * weight_own
+        )
+        for side in range(2):
+            for s in range(samples):
+                first = side * core_rows + s * rows
+                target = (s * KEY_VALUE_HEADS + 2 * at + side) * rows
+                out_ref[pl.ds(target, rows), :] = result[first : first + rows].astype(
+                    out_ref.dtype
                 )
-            turned = jnp.concatenate([top, below, jnp.zeros((6, chip_rows), F32)], axis=0).T
-            peak, total = turned[:, 0:1], turned[:, 1:2]
-            at = half * (HALF // 2) + pair
-            top = jnp.maximum(peak, suffix_max[at])
-            weight = jnp.exp2((peak - top) * FACTOR)
-            weight_own = jnp.exp2((suffix_max[at] - top) * FACTOR)
-            result = (above.T * weight + suffix_out[at] * weight_own) / (
-                total * weight + suffix_total[at] * weight_own
-            )
-            for side in range(2):
-                for s in range(samples):
-                    first = side * core_rows + s * rows
-                    target = (s * KEY_VALUE_HEADS + 2 * at + side) * rows
-                    out_ref[pl.ds(target, rows), :] = result[first : first + rows].astype(
-                        out_ref.dtype
-                    )
-
-    sent = query_buf.at[pl.ds(0, n - 1)]
+
+    for at in range(2 * (HALF // 2)):
+        keep(
+            at,
+            jnp.zeros((HEAD_SIZE, chip_rows), F32),
+            jnp.full((1, chip_rows), -1e30, F32),
+            jnp.zeros((1, chip_rows), F32),
+        )
+
+    def add(step, carry):
+        tiles(lax.rem(last + 1 + step, lines), keep)
+        return carry
+
+    lax.fori_loop(0, lines - 1, add, 0)
+    tiles(last, finish)
+
+    sent = query_buf.at[pl.ds(0, 6 * couples + 1)]
     pltpu.make_async_copy(sent, sent, query_send).wait()
+    sent = query_buf.at[pl.ds(0, 4)]
+    for turn in range(1, couples):
+
+        @pl.when(gateway(turn))
+        def _():
+            pltpu.make_async_copy(sent, sent, forward_sem.at[turn]).wait()
+
     pltpu.make_async_copy(y_send, y_send, y_send_sem).wait()
     pltpu.make_async_copy(y_send_stat, y_send_stat, y_stat_sem).wait()
     sent = z_send.at[pl.ds(0, 4 * lines - 2)]
     pltpu.make_async_copy(sent, sent, z_send_sem).wait()
-    sent = z_send_stat.at[pl.ds(0, 2 * lines - 1)]
+    sent = z_send_stat.at[pl.ds(0, 4 * lines - 2)]
     pltpu.make_async_copy(sent, sent, z_stat_sem).wait()
     for copy in swaps:
         copy.wait_send()
@@ -543,9 +629,11 @@
             pltpu.VMEM((lines, HALF, HEAD_SIZE, chip_rows), I16),
             pltpu.VMEM((lines, pairs, 8, chip_rows), F32),
             pltpu.VMEM((lines * 2 * pairs, HEAD_SIZE, chip_rows), I16),
-            pltpu.VMEM((lines * 2, 8, chip_rows), F32),
+            pltpu.VMEM((lines * 2 * pairs, 4, chip_rows), F32),
             pltpu.VMEM((lines, 2, pairs, HEAD_SIZE, chip_rows), I16),
-            pltpu.VMEM((lines, 2, 8, chip_rows), F32),
+            pltpu.VMEM((lines, 2, pairs, 4, chip_rows), F32),
+            pltpu.VMEM((2 * pairs, HEAD_SIZE, chip_rows), F32),
+            pltpu.VMEM((2 * pairs, 8, chip_rows), F32),
             pltpu.VMEM((2 * pairs, 2 * core_rows, HEAD_SIZE), F32),
             pltpu.VMEM((2 * pairs, 2 * core_rows, 1), F32),
             pltpu.VMEM((2 * pairs, 2 * core_rows, 1), F32),
@@ -553,6 +641,7 @@
             dma((2,)),
             dma((2,)),
             dma,
+            dma((lines // 2,)),
             dma((n,)),
             dma,
             dma,
@@ -561,7 +650,7 @@
             dma,
             dma,
             dma((lines, 2, pairs)),
-            dma((lines, 2)),
+            dma((lines, 2, pairs)),
         ],
         compiler_params=pltpu.CompilerParams(
             collective_id=0, has_side_effects=True, vmem_limit_bytes=60 << 20

time: 41.4 us -> 39.8 us (0.961)
  Pallas kernels: 40.2 us -> 39 us
    pallas_call x1, Pallas kernels: 40.2 us -> 39 us  [body(): pl.pallas_call(functools.partial(kernel, n), out_shape=pltpu.VMEM((sample...]
where the time goes in v4:
time: 39.8 us; the launch traced here: 39.7 us
  Pallas kernels  39 us (98%)
  local copies, waits for them, and re-layouts  0.66 us (2%)
    pallas_call x1, Pallas kernels, body(): pl.pallas_call(functools.partial(kernel, n), out_shape=pltpu.VMEM((sample...  39 us

profile of v4, /device:TPU:0, one launch (start us, length us, event | category | flops | bytes accessed | tf_op | source)
XLA Modules:
  0.0 39.7 jit_solution(9477434515199873303)
XLA Ops:
  0.0 39.0 %shard_map.91 = bf16[512,128]{1,0:T(8,128)(2,1)S(1)} custom-call(s32[2]{0:T(128)} %lengths.1, s32[2]{0:T(128)} %prompt_id.1, bf16[2,4,8192]{2,1,0:T(4,128)(2,1)} %queries.1, bf16[2,4,1024]{2,1,0:T(4,128)(2,1)} %step_keys.1, bf16[2,4,1024]{2,1,0:T(4,128)(2,1)} %step_values.1, bf16[2,1024,1024]{2,1,0:T(8,128)(2,1)} %sample_keys.1, ...), custom_call_target="tpu_custom_call" | custom-call | tf_op jit(solution)/shard_map/pallas_call | solution.py:606
  39.0 0.7 %copy.12 = bf16[2,4,8192]{2,1,0:T(4,128)(2,1)} copy(bf16[2,4,8192]{2,1,0:T(4,128)(2,1)S(1)} %bitcast.5) | data formatting | bytes 262144

commit v5 on v4

--- a/solution.py
+++ b/solution.py
@@ -14,7 +14,6 @@
 GROUP = QUERY_HEADS // KEY_VALUE_HEADS
 LOG2E = 1.4426950408889634
 FACTOR = (HEAD_SIZE ** (-0.5)) * LOG2E
-ID_ROWS = 16
 LEVELS = 32767.0
 MESH = pl.DeviceIdType.MESH
 NT = (((1,), (1,)), ((), ()))
@@ -52,6 +51,8 @@
     query_msg,
     query_pair,
     query_buf,
+    mark_msg,
+    mark_buf,
     own_part,
     own_stat,
     y_send,
@@ -73,6 +74,8 @@
     query_send,
     forward_sem,
     query_recv,
+    mark_send,
+    mark_recv,
     y_send_sem,
     y_stat_sem,
     y_recv,
@@ -136,6 +139,10 @@
     def arrived(ref, sem):
         pltpu.make_async_copy(ref, ref, sem).wait()
 
+    def query_arrived(source):
+        arrived(query_buf.at[source], query_recv.at[source])
+        arrived(mark_buf.at[source], mark_recv.at[source])
+
     partner = device(line, row, 1 - core)
     across = device(line, 1 - row, core)
 
@@ -148,12 +155,19 @@
     for c in range(2):
         greet(device(line, 1 - row, c))
 
-    def greet_line(step, carry):
-        for c in range(2):
-            greet(device(lax.rem(line + step, lines), row, c))
+    for c in range(2):
+        greet(device(mate, row, c))
+
+    def greet_far(turn, carry):
+        @pl.when(gateway(turn))
+        def _():
+            for at in range(2):
+                for c in range(2):
+                    greet(device(couple_at(turn) * 2 + at, row, c))
+
         return carry
 
-    lax.fori_loop(1, lines, greet_line, 0)
+    lax.fori_loop(1, couples, greet_far, 0)
 
     def half_of(ref, half):
         return ref.at[:, :, pl.ds(pl.multiple_of(half * half_width, half_width), half_width)]
@@ -195,20 +209,17 @@
                 g // 2, s, pl.ds(side * rows, rows), pl.ds(side * HEAD_SIZE, HEAD_SIZE)
             ] = part
     small[3].wait()
-    tile_row = lax.broadcasted_iota(jnp.int32, (ID_ROWS, HEAD_SIZE), 0)
-    tile_lane = lax.broadcasted_iota(jnp.int32, (ID_ROWS, HEAD_SIZE), 1)
-    tile_sample = lax.rem(tile_lane, core_rows) // rows
-    marks = jnp.zeros((ID_ROWS, HEAD_SIZE), F32)
+    mark_lane = lax.rem(lax.broadcasted_iota(jnp.int32, (1, HEAD_SIZE), 1), core_rows) // rows
+    marks = jnp.zeros((1, HEAD_SIZE), F32)
     for s in range(samples):
-        mine = (tile_row == s) | ((tile_row >= samples) & (tile_sample == s))
-        marks = jnp.where(mine, id_ref[s].astype(F32), marks)
-    for half in range(2):
-        query_msg[half, pl.ds(HALF * core_rows, ID_ROWS), :] = marks.astype(BF16)
-
-    pl.semaphore_wait(barrier, 2 * lines + 1)
+        marks = jnp.where(mark_lane == s, id_ref[s].astype(F32), marks)
+    mark_msg[...] = marks
+
+    pl.semaphore_wait(barrier, 2 * couples + 3)
 
     def send_query(half, other):
         remote(query_msg.at[half], query_buf.at[me], query_send, query_recv.at[me], other).start()
+        remote(mark_msg, mark_buf.at[me], mark_send, mark_recv.at[me], other).start()
 
     for c in range(2):
         send_query(c, device(line, 1 - row, c))
@@ -233,6 +244,7 @@
         copy.start()
 
     query_buf[me] = query_msg[core]
+    mark_buf[me] = marks
     small[1].wait()
     small[2].wait()
     small[4].wait()
@@ -289,7 +301,7 @@
     def relay(step):
         for c in range(2):
             source = device(line_at(step), row, c)
-            arrived(query_buf.at[source], query_recv.at[source])
+            query_arrived(source)
             turn = turn_at(step)
 
             @pl.when(gateway(turn))
@@ -297,8 +309,15 @@
                 remote(
                     query_buf.at[source],
                     query_buf.at[source],
-                    forward_sem.at[turn],
+                    forward_sem.at[0, turn],
                     query_recv.at[source],
+                    device(mate, row, core),
+                ).start()
+                remote(
+                    mark_buf.at[source],
+                    mark_buf.at[source],
+                    forward_sem.at[1, turn],
+                    mark_recv.at[source],
                     device(mate, row, core),
                 ).start()
 
@@ -309,6 +328,13 @@
                 query_recv.at[source],
                 across,
             ).start()
+            remote(
+                mark_buf.at[source],
+                mark_buf.at[source],
+                mark_send,
+                mark_recv.at[source],
+                across,
+            ).start()
 
     def attend(step):
         there = line_at(step)
@@ -317,22 +343,20 @@
 
         @pl.when(step == 0)
         def _():
-            arrived(query_buf.at[partner], query_recv.at[partner])
+            query_arrived(partner)
 
         for source in theirs:
-            arrived(query_buf.at[source], query_recv.at[source])
+            query_arrived(source)
         sources = mine + theirs
-        tiles = [
-            query_buf[source, pl.ds(HALF * core_rows, ID_ROWS), :].astype(F32)
-            for source in sources
-        ]
+        marked = [mark_buf[source] for source in sources]
         masks = [
             jnp.concatenate(
                 [
                     jnp.broadcast_to(
-                        jnp.where(tile[s : s + 1] == p, 1.0, 0.0), (rows, HEAD_SIZE)
+                        jnp.where(mark[:, s * rows : s * rows + 1] == p, 1.0, 0.0),
+                        (rows, HEAD_SIZE),
                     )
-                    for tile in tiles
+                    for mark in marked
                     for s in range(samples)
                 ],
                 axis=0,
@@ -341,11 +365,7 @@
         ]
         marks = jnp.concatenate(
             [
-                jnp.where(
-                    lane < core_rows,
-                    tiles[2 * k][samples : samples + 1],
-                    tiles[2 * k + 1][samples : samples + 1],
-                )
+                jnp.where(lane < core_rows, marked[2 * k], marked[2 * k + 1])
                 for k in range(2)
             ],
             axis=1,
@@ -377,9 +397,8 @@
                 own_stat[step, h, 1:2, :] = total[:, :chip_rows]
                 y_send[step, h], scale = quantize(result[:, chip_rows:])
                 stats += [peak[:, chip_rows:], total[:, chip_rows:], scale]
-            y_send_stat[step, pair] = jnp.concatenate(
-                stats + [jnp.zeros((2, chip_rows), F32)], axis=0
-            )
+            for k, stat in enumerate(stats):
+                y_send_stat[step, pair, k % 3, k // 3 : k // 3 + 1, :] = stat
             heads = pl.ds(2 * pair, 2)
             remote(
                 y_send.at[step, heads],
@@ -412,14 +431,11 @@
             arrived(y_got.at[step, pl.ds(2 * pair, 2)], y_recv.at[step, pair])
             arrived(y_got_stat.at[step, pair], y_stat_recv.at[step, pair])
             merged = []
-            got = y_got_stat[step, pair]
             for side in range(2):
                 h = 2 * pair + side
                 peak_a, total_a = own_stat[step, h, 0:1, :], own_stat[step, h, 1:2, :]
                 peak_b, total_b, scale_b = (
-                    got[3 * side : 3 * side + 1],
-                    got[3 * side + 1 : 3 * side + 2],
-                    got[3 * side + 2 : 3 * side + 3],
+                    y_got_stat[step, pair, k, side : side + 1, :] for k in range(3)
                 )
                 top = jnp.maximum(peak_a, peak_b)
                 weight_a = jnp.exp2((peak_a - top) * FACTOR)
@@ -462,7 +478,7 @@
                 )
 
     def attend_at(trip):
-        outer = jnp.where(upper & (trip >= 2), trip + 1 - 2 * lax.rem(trip, 2), trip + 0)
+        outer = jnp.where(upper & (jnp.where(trip == 0, 0, trip + 1) >= 2) & (trip < lines - 1), trip + 2 - 2 * lax.rem(trip + 1, 2), jnp.where(trip == 0, 0, jnp.where(trip == lines - 1, 1, trip + 1)))
         return jnp.where(inner, jnp.where(trip <= lines - 3, trip + 2, trip + 2 - lines), outer)
 
     def relay_at(index):
@@ -470,15 +486,23 @@
         return jnp.where(inner, jnp.where(index <= lines - 3, index + 2, 1), outer)
 
     def advance(trip, carry):
-        @pl.when((trip == 0) == inner)
-        def _():
-            @pl.when(trip <= 1)
-            def _():
-                relay(relay_at(1))
-
-        @pl.when((trip >= 1) & (trip <= HALF // 2))
-        def _():
-            suffix(trip + HALF // 2 - 1)
+        turned = ((trip == 0) == inner) & (trip <= 1)
+
+        @pl.when(turned)
+        def _():
+            suffix(HALF // 2)
+
+        @pl.when(turned & inner)
+        def _():
+            suffix(HALF // 2 + 1)
+
+        @pl.when(turned)
+        def _():
+            relay(relay_at(1))
+
+        @pl.when(turned & jnp.logical_not(inner))
+        def _():
+            suffix(HALF // 2 + 1)
 
         index = trip + 1 - jnp.where(inner, 1, 0)
 
@@ -558,14 +582,13 @@
     lax.fori_loop(0, lines - 1, add, 0)
     tiles(last, finish)
 
-    sent = query_buf.at[pl.ds(0, 6 * couples + 1)]
-    pltpu.make_async_copy(sent, sent, query_send).wait()
-    sent = query_buf.at[pl.ds(0, 4)]
-    for turn in range(1, couples):
-
-        @pl.when(gateway(turn))
-        def _():
-            pltpu.make_async_copy(sent, sent, forward_sem.at[turn]).wait()
+    for kind, (buf, sem) in enumerate(((query_buf, query_send), (mark_buf, mark_send))):
+        arrived(buf.at[pl.ds(0, 6 * couples + 1)], sem)
+        for turn in range(1, couples):
+
+            @pl.when(gateway(turn))
+            def _():
+                arrived(buf.at[pl.ds(0, 4)], forward_sem.at[kind, turn])
 
     pltpu.make_async_copy(y_send, y_send, y_send_sem).wait()
     pltpu.make_async_copy(y_send_stat, y_send_stat, y_stat_sem).wait()
@@ -619,15 +642,17 @@
             pltpu.VMEM((prompts, 2 * block, half_width), BF16),
             pltpu.VMEM((prompts, 2 * block, half_width), BF16),
             pltpu.VMEM((HALF, prompts * HEAD_SIZE, 2 * block), BF16),
-            pltpu.VMEM((2, HALF * core_rows + ID_ROWS, HEAD_SIZE), BF16),
+            pltpu.VMEM((2, HALF * core_rows, HEAD_SIZE), BF16),
             pltpu.VMEM((2 * pairs, samples, 2 * rows, 2 * HEAD_SIZE), BF16),
-            pltpu.VMEM((n, HALF * core_rows + ID_ROWS, HEAD_SIZE), BF16),
+            pltpu.VMEM((n, HALF * core_rows, HEAD_SIZE), BF16),
+            pltpu.VMEM((1, HEAD_SIZE), F32),
+            pltpu.VMEM((n, 1, HEAD_SIZE), F32),
             pltpu.VMEM((lines, HALF, HEAD_SIZE, chip_rows), F32),
             pltpu.VMEM((lines, HALF, 8, chip_rows), F32),
             pltpu.VMEM((lines, HALF, HEAD_SIZE, chip_rows), I16),
-            pltpu.VMEM((lines, pairs, 8, chip_rows), F32),
+            pltpu.VMEM((lines, pairs, 3, 2, chip_rows), F32),
             pltpu.VMEM((lines, HALF, HEAD_SIZE, chip_rows), I16),
-            pltpu.VMEM((lines, pairs, 8, chip_rows), F32),
+            pltpu.VMEM((lines, pairs, 3, 2, chip_rows), F32),
             pltpu.VMEM((lines * 2 * pairs, HEAD_SIZE, chip_rows), I16),
             pltpu.VMEM((lines * 2 * pairs, 4, chip_rows), F32),
             pltpu.VMEM((lines, 2, pairs, HEAD_SIZE, chip_rows), I16),
@@ -641,7 +666,9 @@
             dma((2,)),
             dma((2,)),
             dma,
-            dma((lines // 2,)),
+            dma((2, lines // 2)),
+            dma((n,)),
+            dma,
             dma((n,)),
             dma,
             dma,

time: 39.8 us -> 38.9 us (0.977); the launches traced: 39.7 us -> 38.2 us
  Pallas kernels: 39 us -> 37.5 us
    pallas_call x1, Pallas kernels: 39 us -> 37.5 us  [body(): pl.pallas_call(functools.partial(kernel, n), out_shape=pltpu.VMEM((sample...]
where the time goes in v5:
time: 38.9 us; the launch traced here: 38.2 us
  Pallas kernels  37.5 us (96%)
  local copies, waits for them, and re-layouts  0.66 us (2%)
    pallas_call x1, Pallas kernels, body(): pl.pallas_call(functools.partial(kernel, n), out_shape=pltpu.VMEM((sample...  37.5 us

profile of v5, /device:TPU:0, one launch (start us, length us, event | category | flops | bytes accessed | tf_op | source)
XLA Modules:
  0.0 38.2 jit_solution(12303539037216390346)
XLA Ops:
  0.0 37.5 %shard_map.91 = bf16[512,128]{1,0:T(8,128)(2,1)S(1)} custom-call(s32[2]{0:T(128)} %lengths.1, s32[2]{0:T(128)} %prompt_id.1, bf16[2,4,8192]{2,1,0:T(4,128)(2,1)} %queries.1, bf16[2,4,1024]{2,1,0:T(4,128)(2,1)} %step_keys.1, bf16[2,4,1024]{2,1,0:T(4,128)(2,1)} %step_values.1, bf16[2,1024,1024]{2,1,0:T(8,128)(2,1)} %sample_keys.1, ...), custom_call_target="tpu_custom_call" | custom-call | tf_op jit(solution)/shard_map/pallas_call | solution.py:629
  37.5 0.7 %copy.12 = bf16[2,4,8192]{2,1,0:T(4,128)(2,1)} copy(bf16[2,4,8192]{2,1,0:T(4,128)(2,1)S(1)} %bitcast.5) | data formatting | bytes 262144

commit v6 on v5

--- a/solution.py
+++ b/solution.py
@@ -73,6 +73,7 @@
     doc_recv,
     query_send,
     forward_sem,
+    hop_sem,
     query_recv,
     mark_send,
     mark_recv,
@@ -139,9 +140,10 @@
     def arrived(ref, sem):
         pltpu.make_async_copy(ref, ref, sem).wait()
 
-    def query_arrived(source):
-        arrived(query_buf.at[source], query_recv.at[source])
-        arrived(mark_buf.at[source], mark_recv.at[source])
+    def query_arrived(source, pair):
+        if pair == 0:
+            arrived(mark_buf.at[source], mark_recv.at[source])
+        arrived(query_buf.at[source, pair], query_recv.at[source, pair])
 
     partner = device(line, row, 1 - core)
     across = device(line, 1 - row, core)
@@ -203,7 +205,9 @@
                 ],
                 axis=0,
             ).astype(BF16)
-            query_msg[g // HALF, pl.ds((g % HALF) * core_rows + s * rows, rows), :] = part
+            query_msg[
+                g // HALF, (g % HALF) // 2, pl.ds((g % 2) * core_rows + s * rows, rows), :
+            ] = part
             side = g % 2
             query_pair[
                 g // 2, s, pl.ds(side * rows, rows), pl.ds(side * HEAD_SIZE, HEAD_SIZE)
@@ -217,23 +221,32 @@
 
     pl.semaphore_wait(barrier, 2 * couples + 3)
 
-    def send_query(half, other):
-        remote(query_msg.at[half], query_buf.at[me], query_send, query_recv.at[me], other).start()
-        remote(mark_msg, mark_buf.at[me], mark_send, mark_recv.at[me], other).start()
-
-    for c in range(2):
-        send_query(c, device(line, 1 - row, c))
-
-    for c in range(2):
-        send_query(c, device(mate, row, c))
+    def send_query(half, pair, other):
+        if pair == 0:
+            remote(mark_msg, mark_buf.at[me], mark_send, mark_recv.at[me], other).start()
+        remote(
+            query_msg.at[half, pair],
+            query_buf.at[me, pair],
+            query_send,
+            query_recv.at[me, pair],
+            other,
+        ).start()
+
+    def send_chip(at_line, at_row):
+        for pair in range(HALF // 2):
+            for c in range(2):
+                send_query(c, pair, device(at_line, at_row, c))
+
+    send_chip(line, 1 - row)
+    send_chip(mate, row)
 
     def send_far(turn, carry):
-        for c in range(2):
-            send_query(c, device(couple_at(turn) * 2 + wraps(turn), row, c))
+        send_chip(couple_at(turn) * 2 + wraps(turn), row)
         return carry
 
     lax.fori_loop(1, couples, send_far, 0)
-    send_query(1 - core, partner)
+    for pair in range(HALF // 2):
+        send_query(1 - core, pair, partner)
     swaps = [
         remote(half_of(source, 1 - core), own_rows(target), doc_send.at[k], doc_recv.at[k], partner)
         for k, (source, target) in enumerate(
@@ -298,83 +311,127 @@
 
     lane = lax.broadcasted_iota(jnp.int32, (1, chip_rows), 1)
 
+    def pass_on(source, pair, query_sem, mark_sem, other):
+        if pair == 0:
+            remote(
+                mark_buf.at[source], mark_buf.at[source], mark_sem, mark_recv.at[source], other
+            ).start()
+        remote(
+            query_buf.at[source, pair],
+            query_buf.at[source, pair],
+            query_sem,
+            query_recv.at[source, pair],
+            other,
+        ).start()
+
+    def is_far(step):
+        return (step >= 2) & (lax.rem(step, 2) == 1)
+
     def relay(step):
-        for c in range(2):
-            source = device(line_at(step), row, c)
-            query_arrived(source)
-            turn = turn_at(step)
-
-            @pl.when(gateway(turn))
-            def _():
-                remote(
-                    query_buf.at[source],
-                    query_buf.at[source],
+        turn = turn_at(step)
+        sources = [device(line_at(step), row, c) for c in range(2)]
+        for pair in range(HALF // 2):
+            for source in sources:
+                query_arrived(source, pair)
+
+                @pl.when(gateway(turn))
+                def _():
+                    pass_on(
+                        source,
+                        pair,
+                        forward_sem.at[0, turn],
+                        forward_sem.at[1, turn],
+                        device(mate, row, core),
+                    )
+
+                @pl.when(jnp.logical_not(is_far(step)))
+                def _():
+                    pass_on(source, pair, query_send, mark_send, across)
+
+    def hop_out():
+        for pair in range(HALF // 2):
+            for c in range(2):
+                source = device(line, 1 - row, c)
+                query_arrived(source, pair)
+                for turn in range(1, couples):
+
+                    @pl.when(jnp.logical_not(gateway(turn)))
+                    def _():
+                        pass_on(
+                            source,
+                            pair,
+                            hop_sem.at[0, turn],
+                            hop_sem.at[1, turn],
+                            device(couple_at(turn) * 2 + wraps(turn), row, core),
+                        )
+
+    def hop_on(step):
+        turn = turn_at(step)
+        for pair in range(HALF // 2):
+            for c in range(2):
+                source = device(line_at(step), 1 - row, c)
+                query_arrived(source, pair)
+                pass_on(
+                    source,
+                    pair,
                     forward_sem.at[0, turn],
-                    query_recv.at[source],
+                    forward_sem.at[1, turn],
                     device(mate, row, core),
-                ).start()
-                remote(
-                    mark_buf.at[source],
-                    mark_buf.at[source],
-                    forward_sem.at[1, turn],
-                    mark_recv.at[source],
-                    device(mate, row, core),
-                ).start()
-
-            remote(
-                query_buf.at[source],
-                query_buf.at[source],
-                query_send,
-                query_recv.at[source],
-                across,
-            ).start()
-            remote(
-                mark_buf.at[source],
-                mark_buf.at[source],
-                mark_send,
-                mark_recv.at[source],
-                across,
-            ).start()
+                )
 
     def attend(step):
         there = line_at(step)
         mine = [device(there, row, c) for c in range(2)]
         theirs = [device(there, 1 - row, c) for c in range(2)]
 
-        @pl.when(step == 0)
-        def _():
-            query_arrived(partner)
-
-        for source in theirs:
-            query_arrived(source)
         sources = mine + theirs
-        marked = [mark_buf[source] for source in sources]
-        masks = [
-            jnp.concatenate(
-                [
-                    jnp.broadcast_to(
-                        jnp.where(mark[:, s * rows : s * rows + 1] == p, 1.0, 0.0),
-                        (rows, HEAD_SIZE),
-                    )
-                    for mark in marked
-                    for s in range(samples)
-                ],
-                axis=0,
-            ).astype(BF16)
-            for p in range(prompts)
-        ]
-        marks = jnp.concatenate(
-            [
-                jnp.where(lane < core_rows, marked[2 * k], marked[2 * k + 1])
-                for k in range(2)
-            ],
-            axis=1,
-        )
+        hopped = is_far(step) & gateway(turn_at(step))
+
+        @pl.when(hopped)
+        def _():
+            hop_on(step)
+
         for pair in range(HALF // 2):
+
+            @pl.when(step == 0)
+            def _():
+                query_arrived(partner, pair)
+
+            @pl.when((step != 0) & jnp.logical_not(hopped))
+            def _():
+                for source in theirs:
+                    query_arrived(source, pair)
+
+            if pair == 0:
+                marked = [mark_buf[source] for source in sources]
+                masks = [
+                    jnp.concatenate(
+                        [
+                            jnp.broadcast_to(
+                                jnp.where(mark[:, s * rows : s * rows + 1] == p, 1.0, 0.0),
+                                (rows, HEAD_SIZE),
+                            )
+                            for mark in marked
+                            for s in range(samples)
+                        ],
+                        axis=0,
+                    ).astype(BF16)
+                    for p in range(prompts)
+                ]
+                marks = jnp.concatenate(
+                    [
+                        jnp.where(lane < core_rows, marked[2 * k], marked[2 * k + 1])
+                        for k in range(2)
+                    ],
+                    axis=1,
+                )
             stats = []
             for h in (2 * pair, 2 * pair + 1):
                 query = jnp.concatenate(
-                    [query_buf[source, pl.ds(h * core_rows, core_rows), :] for source in sources],
+                    [
+                        query_buf[source, pair, pl.ds((h % 2) * core_rows, core_rows), :]
+                        for source in sources
+                    ],
                     axis=0,
                 )
                 query = jnp.concatenate([query * mask for mask in masks], axis=1)
@@ -477,9 +534,19 @@
                     device(there, row, c),
                 )
 
+    far = list(range(2, lines))
+    swapped = [step + 1 - 2 * (step % 2) for step in far]
+
+    def pick(order, trip):
+        chosen = order[-1]
+        for k in range(lines - 1):
+            chosen = jnp.where(trip == k, order[k], chosen)
+        return chosen
+
     def attend_at(trip):
-        outer = jnp.where(upper & (jnp.where(trip == 0, 0, trip + 1) >= 2) & (trip < lines - 1), trip + 2 - 2 * lax.rem(trip + 1, 2), jnp.where(trip == 0, 0, jnp.where(trip == lines - 1, 1, trip + 1)))
-        return jnp.where(inner, jnp.where(trip <= lines - 3, trip + 2, trip + 2 - lines), outer)
+        low = jnp.where(inner, pick(far + [0, 1], trip), pick([0] + far + [1], trip))
+        high = jnp.where(inner, pick(far + [0, 1], trip), pick([0] + swapped + [1], trip))
+        return jnp.where(upper, high, low)
 
     def relay_at(index):
         outer = index + 1
@@ -519,6 +586,7 @@
         return carry
 
     relay(relay_at(0))
+    hop_out()
     lax.fori_loop(0, lines, advance, 0)
     combine(attend_at(lines - 1))
 
@@ -583,12 +651,16 @@
     tiles(last, finish)
 
     for kind, (buf, sem) in enumerate(((query_buf, query_send), (mark_buf, mark_send))):
-        arrived(buf.at[pl.ds(0, 6 * couples + 1)], sem)
+        arrived(buf.at[pl.ds(0, 4 * couples + 3)], sem)
         for turn in range(1, couples):
 
             @pl.when(gateway(turn))
             def _():
-                arrived(buf.at[pl.ds(0, 4)], forward_sem.at[kind, turn])
+                arrived(buf.at[pl.ds(0, 6)], forward_sem.at[kind, turn])
+
+            @pl.when(jnp.logical_not(gateway(turn)))
+            def _():
+                arrived(buf.at[pl.ds(0, 2)], hop_sem.at[kind, turn])
 
     pltpu.make_async_copy(y_send, y_send, y_send_sem).wait()
     pltpu.make_async_copy(y_send_stat, y_send_stat, y_stat_sem).wait()
@@ -642,9 +714,9 @@
             pltpu.VMEM((prompts, 2 * block, half_width), BF16),
             pltpu.VMEM((prompts, 2 * block, half_width), BF16),
             pltpu.VMEM((HALF, prompts * HEAD_SIZE, 2 * block), BF16),
-            pltpu.VMEM((2, HALF * core_rows, HEAD_SIZE), BF16),
+            pltpu.VMEM((2, pairs, 2 * core_rows, HEAD_SIZE), BF16),
             pltpu.VMEM((2 * pairs, samples, 2 * rows, 2 * HEAD_SIZE), BF16),
-            pltpu.VMEM((n, HALF * core_rows, HEAD_SIZE), BF16),
+            pltpu.VMEM((n, pairs, 2 * core_rows, HEAD_SIZE), BF16),
             pltpu.VMEM((1, HEAD_SIZE), F32),
             pltpu.VMEM((n, 1, HEAD_SIZE), F32),
             pltpu.VMEM((lines, HALF, HEAD_SIZE, chip_rows), F32),
@@ -667,7 +739,8 @@
             dma((2,)),
             dma,
             dma((2, lines // 2)),
-            dma((n,)),
+            dma((2, lines // 2)),
+            dma((n, pairs)),
             dma,
             dma((n,)),
             dma,

time: 38.9 us -> 36.5 us (0.938); the launches traced: 38.2 us -> 36.3 us
  Pallas kernels: 37.5 us -> 35.7 us
    pallas_call x1, Pallas kernels: 37.5 us -> 35.7 us  [body(): pl.pallas_call(functools.partial(kernel, n), out_shape=pltpu.VMEM((sample...]
where the time goes in v6:
time: 36.5 us; the launch traced here: 36.3 us
  Pallas kernels  35.7 us (98%)
  local copies, waits for them, and re-layouts  0.66 us (2%)
    pallas_call x1, Pallas kernels, body(): pl.pallas_call(functools.partial(kernel, n), out_shape=pltpu.VMEM((sample...  35.7 us

profile of v6, /device:TPU:0, one launch (start us, length us, event | category | flops | bytes accessed | tf_op | source)
XLA Modules:
  0.0 36.3 jit_solution(16167427258747587662)
XLA Ops:
  0.0 35.7 %shard_map.91 = bf16[512,128]{1,0:T(8,128)(2,1)S(1)} custom-call(s32[2]{0:T(128)} %lengths.1, s32[2]{0:T(128)} %prompt_id.1, bf16[2,4,8192]{2,1,0:T(4,128)(2,1)} %queries.1, bf16[2,4,1024]{2,1,0:T(4,128)(2,1)} %step_keys.1, bf16[2,4,1024]{2,1,0:T(4,128)(2,1)} %step_values.1, bf16[2,1024,1024]{2,1,0:T(8,128)(2,1)} %sample_keys.1, ...), custom_call_target="tpu_custom_call" | custom-call | tf_op jit(solution)/shard_map/pallas_call | solution.py:701
  35.7 0.7 %copy.12 = bf16[2,4,8192]{2,1,0:T(4,128)(2,1)} copy(bf16[2,4,8192]{2,1,0:T(4,128)(2,1)S(1)} %bitcast.5) | data formatting | bytes 262144

commit v7 on v6

--- a/solution.py
+++ b/solution.py
@@ -544,13 +544,13 @@
         return chosen
 
     def attend_at(trip):
-        low = jnp.where(inner, pick(far + [0, 1], trip), pick([0] + far + [1], trip))
-        high = jnp.where(inner, pick(far + [0, 1], trip), pick([0] + swapped + [1], trip))
+        low = jnp.where(inner, pick(far + [1, 0], trip), pick([0, 1] + far, trip))
+        high = jnp.where(inner, pick(far + [1, 0], trip), pick([0] + swapped[:1] + [1] + swapped[1:], trip))
         return jnp.where(upper, high, low)
 
     def relay_at(index):
-        outer = index + 1
-        return jnp.where(inner, jnp.where(index <= lines - 3, index + 2, 1), outer)
+        within = jnp.where(index == 0, 2, jnp.where(index == 1, 1, index + 1))
+        return jnp.where(inner, within, index + 1)
 
     def advance(trip, carry):
         turned = ((trip == 0) == inner) & (trip <= 1)
@@ -571,7 +571,7 @@
         def _():
             suffix(HALF // 2 + 1)
 
-        index = trip + 1 - jnp.where(inner, 1, 0)
+        index = jnp.where(inner, trip + 2, jnp.where(upper & (trip >= 1), trip + 1, trip))
 
         @pl.when((index >= 2) & (index <= lines - 2))
         def _():

time: 36.5 us -> 35.4 us (0.970)
  Pallas kernels: 35.7 us -> 34.6 us
    pallas_call x1, Pallas kernels: 35.7 us -> 34.6 us  [body(): pl.pallas_call(functools.partial(kernel, n), out_shape=pltpu.VMEM((sample...]
where the time goes in v7:
time: 35.4 us; the launch traced here: 35.2 us
  Pallas kernels  34.6 us (98%)
  local copies, waits for them, and re-layouts  0.66 us (2%)
    pallas_call x1, Pallas kernels, body(): pl.pallas_call(functools.partial(kernel, n), out_shape=pltpu.VMEM((sample...  34.6 us

profile of v7, /device:TPU:0, one launch (start us, length us, event | category | flops | bytes accessed | tf_op | source)
XLA Modules:
  0.0 35.2 jit_solution(5442044173043920804)
XLA Ops:
  0.0 34.6 %shard_map.91 = bf16[512,128]{1,0:T(8,128)(2,1)S(1)} custom-call(s32[2]{0:T(128)} %lengths.1, s32[2]{0:T(128)} %prompt_id.1, bf16[2,4,8192]{2,1,0:T(4,128)(2,1)} %queries.1, bf16[2,4,1024]{2,1,0:T(4,128)(2,1)} %step_keys.1, bf16[2,4,1024]{2,1,0:T(4,128)(2,1)} %step_values.1, bf16[2,1024,1024]{2,1,0:T(8,128)(2,1)} %sample_keys.1, ...), custom_call_target="tpu_custom_call" | custom-call | tf_op jit(solution)/shard_map/pallas_call | solution.py:701
  34.6 0.7 %copy.12 = bf16[2,4,8192]{2,1,0:T(4,128)(2,1)} copy(bf16[2,4,8192]{2,1,0:T(4,128)(2,1)S(1)} %bitcast.5) | data formatting | bytes 262144
